TPU v7x, 256 devices: a whole 4x4x8 slice. The times are simulated.
256 devices in a mesh: req: 32 (over z, y), seq: 8 (over x, core).
Axes of the slice: x: 4, y: 4, z: 8, core: 2. Of those that a mesh axis runs over, the one named last changes fastest.
Arguments:
- tokens: bfloat16 [32, 4096, 2560], P('req', 'seq'), may hold values from -6 to 6
- mix_weight: bfloat16 [2560, 2816], P(('req', 'seq')), may hold values from -0.125 to 0.125
- step_weight: bfloat16 [2560, 40], P(('req', 'seq')), may hold values from -0.125 to 0.125
- conv_weight: float32 [4, 2816], replicated, may hold values from -3 to 3
- conv_bias: float32 [2816], replicated, may hold values from -3 to 3
- step_bias: float32 [40], replicated, may hold values from -5 to -3
- decay_rate: float32 [40], replicated, may hold values from 0.00048828125 to 1
- skip_gain: float32 [40], replicated, may hold values from 0.5 to 2
- norm_gain: float32 [2560], replicated, may hold values from 0.1 to 1.9
- prompt_len: int32 [32], replicated, may hold values from 1024 to 4096, as said below
- prompt_start: int32 [32], replicated, may hold values from 0 to 3072, as said below
- deal: int32 [32], replicated, may hold values from 0 to 31, as said below
Outputs:
- result: bfloat16 [32, 4096, 2560], P('req', 'seq')
- final_state: float32 [32, 40, 64, 128], P('req', 'seq')
Inputs may be any that keep to these rules, and one draw needn't show every extreme that they name: `prompt_len`: one prompt has exactly 4096 positions and one exactly a quarter of 4096. prompt_start plus prompt_len is at most 4096 for every request. `deal`: a permutation of the requests; some slot s holds request (s + 16) modulo 32.
All inputs are finite; a program needn't handle non-finite values.
Results may differ from a plain program's by a relative error of at most 0.0035.
Values may be sent and summed in bfloat16 or wider, within the bound.
A program may use at most 128 MiB of HBM per device.

v0:
```python
import jax
import jax.numpy as jnp
from jax import lax
from jax.sharding import PartitionSpec as P

GROUP = 256


EPS = 1e-05


def passed_along(block, axis, distance):
    devices = range(lax.axis_size(axis))
    route = [(i - distance, i) for i in devices if i - distance in devices]
    return lax.ppermute(block, axis, route)


def carried_in(part, axis, combine, identity):
    place = lax.axis_index(axis)
    gathered = jax.tree.map(lambda a: lax.all_gather(a, axis), part)
    state = jax.tree.map(lambda a, e: jnp.zeros_like(a) + jnp.asarray(e, a.dtype), part, identity)

    def one(step, state):
        return combine(
            state, jax.tree.map(lambda a: lax.dynamic_index_in_dim(a, step, 0, False), gathered)
        )

    return lax.fori_loop(0, place, one, state)


def broadcast(x, axis, root):
    mine = lax.axis_index(axis) == root
    return lax.psum(jnp.where(mine, x, jnp.zeros_like(x)), axis)


def on_device(
    tokens,
    mix_weight,
    step_weight,
    conv_weight,
    conv_bias,
    step_bias,
    decay_rate,
    skip_gain,
    norm_gain,
    prompt_len,
    prompt_start,
    deal,
):
    seq_count = lax.axis_size("seq")
    seq_index = lax.axis_index("seq")
    req_index = lax.axis_index("req")
    rows = tokens[0]
    span = rows.shape[0]
    total_reqs = deal.shape[0]
    slots = jnp.arange(total_reqs, dtype=jnp.int32)
    request = jnp.sum(jnp.where(slots == req_index, deal, 0))
    length = jnp.sum(jnp.where(slots == request, prompt_len, 0))
    start = jnp.sum(jnp.where(slots == request, prompt_start, 0))
    place = seq_index * span + jnp.arange(span, dtype=jnp.int32)
    valid = ((place >= start) & (place < start + length)).astype(jnp.float32)
    whole_mix, whole_step = (
        lax.all_gather(mix_weight, ("req", "seq"), axis=0, tiled=True),
        lax.all_gather(step_weight, ("req", "seq"), axis=0, tiled=True),
    )
    mixed = jnp.dot(rows, whole_mix, preferred_element_type=jnp.float32)
    raw_step = jnp.dot(rows, whole_step, preferred_element_type=jnp.float32)
    mixed = (mixed * valid[:, None]).astype(jnp.bfloat16)
    taps = conv_weight.shape[0]
    edge = passed_along(mixed[span - (taps - 1) :], "seq", 1)
    padded = jnp.concatenate([edge, mixed], axis=0)
    conv_sum = jnp.zeros(mixed.shape, jnp.float32) + conv_bias[None, :]
    for offset in range(taps):
        conv_sum = conv_sum + conv_weight[offset][None, :] * padded[offset : offset + span].astype(
            jnp.float32
        )
    convolved = jax.nn.silu(conv_sum).astype(jnp.bfloat16)
    heads = decay_rate.shape[0]
    inner = norm_gain.shape[0]
    head_dim = inner // heads
    nstate = (mixed.shape[1] - inner) // 2
    blocks = span // GROUP
    inputs = convolved[:, :inner].reshape(span, heads, head_dim)
    mixed_b = convolved[:, inner : inner + nstate]
    mixed_c = convolved[:, inner + nstate :]
    step_size = jax.nn.softplus(raw_step + step_bias[None, :]) * valid[:, None]
    pieces = (
        inputs.reshape(blocks, GROUP, heads, head_dim),
        mixed_b.reshape(blocks, GROUP, nstate),
        mixed_c.reshape(blocks, GROUP, nstate),
        step_size.reshape(blocks, GROUP, heads),
    )

    def local_group(block):
        part_in, part_b, part_c, part_step = block
        cum_decay = jnp.cumsum(-part_step * decay_rate[None, :], axis=0)
        places = jnp.arange(GROUP, dtype=jnp.int32)
        causal = places[:, None] >= places[None, :]
        spread = cum_decay[:, None, :] - cum_decay[None, :, :]
        spread = jnp.where(causal[:, :, None], spread, -1e30)
        scores = jnp.einsum("qn,kn->qk", part_c, part_b, preferred_element_type=jnp.float32)
        mixing = (jnp.exp(spread) * scores[:, :, None] * part_step[None, :, :]).astype(jnp.bfloat16)
        inner_out = jnp.einsum("qkh,khp->qhp", mixing, part_in, preferred_element_type=jnp.float32)
        to_end = jnp.exp(cum_decay[-1][None, :] - cum_decay) * part_step
        scaled = (to_end[:, :, None] * part_in.astype(jnp.float32)).astype(jnp.bfloat16)
        local = jnp.einsum("khp,kn->hpn", scaled, part_b, preferred_element_type=jnp.float32)
        return (inner_out, cum_decay, local)

    inner_out, cum_decay, group_state = lax.map(local_group, pieces)
    totals = cum_decay[:, -1, :]

    def advance(carry, item):
        group_total, group_local = item
        return (jnp.exp(group_total)[:, None, None] * carry + group_local, carry)

    dev_state, entry_zero = lax.scan(
        advance, jnp.zeros((heads, head_dim, nstate), jnp.float32), (totals, group_state)
    )
    before = jnp.cumsum(totals, axis=0) - totals
    dev_decay = jnp.exp(jnp.sum(totals, axis=0))

    def chain(earlier, later):
        return (earlier[0] * later[0], later[0][:, None, None] * earlier[1] + later[1])

    incoming_decay, incoming = carried_in(
        (dev_decay, dev_state), "seq", chain, (jnp.ones_like(dev_decay), jnp.zeros_like(dev_state))
    )
    entry = entry_zero + jnp.exp(before)[:, :, None, None] * incoming[None]
    carried = jnp.einsum(
        "cqn,chpn->cqhp", pieces[2].astype(jnp.float32), entry, precision=lax.Precision.HIGHEST
    )
    carried = carried * jnp.exp(cum_decay)[:, :, :, None]
    outputs = (inner_out + carried).reshape(span, heads, head_dim) + skip_gain[
        None, :, None
    ] * inputs.astype(jnp.float32)
    flat = outputs.reshape(span, inner)
    factor = lax.rsqrt(jnp.mean(flat * flat, axis=1, keepdims=True) + EPS)
    result = (flat * factor * norm_gain[None, :] * valid[:, None]).astype(jnp.bfloat16)[None]
    share = heads // seq_count
    leaving = dev_decay[:, None, None] * incoming + dev_state
    last_state = broadcast(leaving, "seq", seq_count - 1)
    own_state = lax.dynamic_slice_in_dim(last_state, seq_index * share, share, 0)[None]
    wanted = jnp.sum(jnp.where(deal == req_index, slots, 0))
    piece = lax.all_gather(own_state, "req", axis=0, tiled=True)
    count = piece.shape[0]
    chosen = jnp.arange(count, dtype=jnp.int32) == wanted
    final_state = jnp.zeros_like(own_state) + jnp.sum(
        jnp.where(chosen[:, None, None, None], piece, 0.0), axis=0, keepdims=True
    )
    return (result, final_state)


def solution(mesh):
    return jax.shard_map(
        on_device,
        mesh=mesh,
        in_specs=(
            P("req", "seq", None),
            P(("req", "seq"), None),
            P(("req", "seq"), None),
            P(),
            P(),
            P(),
            P(),
            P(),
            P(),
            P(),
            P(),
            P(),
        ),
        out_specs=(P("req", "seq", None), P("req", "seq", None, None)),
        check_vma=False,
    )
```

profile of v0, /device:TPU:2, one launch (start us, length us, event | category | flops | bytes accessed | tf_op | source)
XLA Modules:
  0.0 482.0 jit_solution(1051136293453293092)
XLA Ops:
  8.0 70.5 %all-gather.4 = bf16[256,10,40]{2,1,0:T(8,128)(2,1)} all-gather(bf16[1,10,40]{2,1,0:T(8,128)(2,1)} %bitcast.158), channel_id=1, replica_groups=mesh['req'=32,'seq'=8] {'req','seq'}, dimensions={0}, use_global_device_ids=true | all-gather | bytes 205600 | tf_op jit(solution)/shard_map/all_gather | solution.py:64
  81.3 1.9 fusion.51
  83.2 2.0 fusion.52
  88.7 60.2 %all-gather.13.cloned.1.call-done = bf16[256,10,2816]{2,1,0:T(8,128)(2,1)} async-done(((bf16[1,10,2816]{2,1,0:T(8,128)(2,1)}), bf16[256,10,2816]{2,1,0:T(8,128)(2,1)}) %all-gather.13.cloned.1.call-update) | async-done | bytes 14417936 | tf_op jit(solution)/shard_map/all_gather | solution.py:63
  149.0 25.3 %reshape.117 = bf16[2560,2816]{1,0:T(8,128)(2,1)} reshape(bf16[256,10,2816]{2,1,0:T(8,128)(2,1)} %all-gather.13.cloned.1.call-done) | data formatting | bytes 28835840
  174.2 11.5 %multiply_convert_fusion.6 = bf16[512,2816]{1,0:T(8,128)(2,1)S(1)} fusion(bf16[2560,2816]{1,0:T(8,128)(2,1)} %reshape.117, f32[512]{0:T(512)S(1)} %fusion.50, bf16[1,512,2560]{2,1,0:T(8,128)(2,1)S(1)} %copy-done), kind=kOutput, calls=%fused_computation.48 | convolution fusion | flops 7384858624 | bytes 19924992 | tf_op jit(solution)/shard_map/dot_general | solution.py:66
  187.4 2.3 collective-permute-start
  189.9 2.6 collective-permute-done
  192.5 7.8 %multiply_convert_fusion.5 = bf16[512,2816]{1,0:T(8,128)(2,1)S(1)} fusion(bf16[512,2816]{1,0:T(8,128)(2,1)} %copy-done.7, bf16[3,2816]{1,0:T(4,128)(2,1)S(1)} %collective-permute-done, f32[2816]{0:T(1024)S(1)} %get-tuple-element.187, f32[2816]{0:T(1024)S(1)} %get-tuple-element.188, f32[2816]{0:T(1024)S(1)} %get-tuple-element.186, ...), kind=kLoop, calls=%fused_computation.47 | loop fusion | flops 37486592 | bytes 5840384 | tf_op jit(solution)/shard_map/convert_element_type | solution.py:77
  201.8 1.7 slice.64
  203.5 7.5 %reshape.124 = bf16[2,256,40,64]{3,2,1,0:T(8,128)(2,1)} reshape(bf16[512,2560]{1,0:T(8,128)(2,1)} %slice.64) | data formatting | bytes 5242880 | tf_op jit(solution)/shard_map/reshape;reshape | solution.py:88
  211.0 6.4 %copy.40 = bf16[2,256,40,64]{1,3,2,0:T(8,128)(2,1)} copy(bf16[2,256,40,64]{3,2,1,0:T(8,128)(2,1)} %reshape.124) | data formatting | bytes 5242880 | tf_op jit(solution)/shard_map/while | solution.py:109
  217.5 1.8 broadcast.58.clone
  219.3 17.0 %while.39 = (s32[]{:T(128)}, f32[2,256,40,64]{1,3,2,0:T(8,128)}, f32[2,256,40]{1,2,0:T(8,128)S(1)}, f32[2,40,64,128]{3,2,1,0:T(8,128)}, bf16[2,256,40,64]{1,3,2,...) while((s32[]{:T(128)}, f32[2,256,40,64]{1,3,2,0:T(8,128)}, ...), condition=%wide.region_6.7_spmd, body=%wide.region_3.6_spmd.sunk | while | flops 536604800 | bytes 18677688 | solution.py:109
  220.5 5.3 %bitcast_dynamic-update-slice_fusion.4 = f32[2,256,40,64]{1,3,2,0:T(8,128)} fusion(f32[2,256,40,64]{1,3,2,0:T(8,128)} %get-tuple-element.363, s32[]{:T(128)} %get-tuple-element.362, f32[256,40]{0,1:T(8,128)S(1)} %bitcast.155, f32[256,256]{1,0:T(8,128)S(1)} %fusion.74, f32[256,40]{0,1:T(8,128)S(1)} %bitcast_bitcast_fusion.3, ...), kind=kOutput, calls=%fused_computation.15.clone.1 | convolution fusion | flops 348651520 | bytes 4383744 | tf_op jit(solution)/shard_map/while/body/eval_jaxpr/qkh,khp->qhp/dot_general | solution.py:103
  226.1 1.6 fusion.76
  229.0 5.3 %bitcast_dynamic-update-slice_fusion.4 = f32[2,256,40,64]{1,3,2,0:T(8,128)} fusion(f32[2,256,40,64]{1,3,2,0:T(8,128)} %get-tuple-element.363, s32[]{:T(128)} %get-tuple-element.362, f32[256,40]{0,1:T(8,128)S(1)} %bitcast.155, f32[256,256]{1,0:T(8,128)S(1)} %fusion.74, f32[256,40]{0,1:T(8,128)S(1)} %bitcast_bitcast_fusion.3, ...), kind=kOutput, calls=%fused_computation.15.clone.1 | convolution fusion | flops 348651520 | bytes 4383744 | tf_op jit(solution)/shard_map/while/body/eval_jaxpr/qkh,khp->qhp/dot_general | solution.py:103
  234.6 1.6 fusion.76
  236.5 1.9 broadcast.58
  238.3 5.6 %while.41 = (s32[]{:T(128)}, f32[40,64,128]{2,1,0:T(8,128)S(1)}, f32[2,40,64,128]{3,2,1,0:T(8,128)}, f32[2,40]{1,0:T(2,128)S(1)}, f32[2,40,64,128]{3,2,1,0:T(8,128)}, /*index=5*/s32[]{:T(128)}, s32[]{:T(128)}) while((s32[]{:T(128)}, f32[40,64,128]{2,1,0:T(8,128)S(1)}, f32[2,40,64,128]{3,2,1,0:T(8,128)}, f32[2,40]{1,0:T(2,128)S(1)}, ...), condition=%wide.region_8.9_spmd.clone, body=%wide.region_7.8_spmd.clone.sunk | while | flops 1310723 | bytes 6554688 | solution.py:116
  246.6 10.0 %all-reduce = f32[320]{0:T(512)S(1)} all-reduce(f32[320]{0:T(512)S(1)} %get-tuple-element.232), channel_id=2, replica_groups=mesh['req'=32,'seq'=8] {'seq'}, use_global_device_ids=true, to_apply=%add | all-reduce | flops 320 | bytes 2560
  256.6 46.0 %all-gather.9.cloned.1.call-done = f32[320,64,128]{2,1,0:T(8,128)} async-done(((f32[40,64,128]{2,1,0:T(8,128)}), f32[320,64,128]{2,1,0:T(8,128)}) %all-gather.9.cloned.1.call-update) | async-done | bytes 10485776 | tf_op jit(solution)/shard_map/all_gather | solution.py:20
  302.8 3.3 while.40
  302.8 1.7 bitcast_add_fusion.4
  307.7 74.1 %all-reduce.3.cloned.1.call-done = f32[40,64,128]{2,1,0:T(8,128)} async-done(((f32[40,64,128]{2,1,0:T(8,128)}), f32[40,64,128]{2,1,0:T(8,128)}) %all-reduce.3.cloned.1.call-update) | async-done | bytes 1310736 | tf_op jit(solution)/shard_map/psum | solution.py:33
  384.3 8.0 %multiply_add_fusion.1 = f32[2,256,40,64]{1,3,2,0:T(8,128)} fusion(f32[2,256,40,64]{1,3,2,0:T(8,128)} %get-tuple-element.123, f32[2,256,40]{1,2,0:T(8,128)S(1)} %exp.56, bf16[2,256,128,1]{2,1,3,0:T(8,128)(2,1)S(1)} %bitcast.154, f32[2,40,64,128]{3,2,1,0:T(8,128)} %get-tuple-element.126, f32[40,64,128]{2,1,0:T(8,128)S(1)} %get-tuple-element.128, ...), kind=kOutput, calls=%fused_computation.53 | convolution fusion | flops 2017198080 | bytes 14631232 | tf_op jit(solution)/shard_map/cqn,chpn->cqhp/dot_general | solution.py:129
  392.4 8.6 %copy.47 = f32[2,256,40,64]{3,2,1,0:T(8,128)} copy(f32[2,256,40,64]{1,3,2,0:T(8,128)} %multiply_add_fusion.1) | data formatting | bytes 10485760 | tf_op jit(solution)/shard_map/reshape | solution.py:133
  401.0 9.6 %reshape.125 = f32[512,2560]{1,0:T(8,128)} reshape(f32[2,256,40,64]{3,2,1,0:T(8,128)} %copy.47) | data formatting | bytes 10485760 | tf_op jit(solution)/shard_map/reshape | solution.py:133
  410.6 4.4 multiply_reduce_fusion
  415.4 4.7 fusion.30
  420.1 51.5 %all-gather.11.cloned.1.call-done = f32[160,64,128]{2,1,0:T(8,128)} async-done(((f32[5,64,128]{2,1,0:T(8,128)}), f32[160,64,128]{2,1,0:T(8,128)}) %all-gather.11.cloned.1.call-update) | async-done | bytes 5242896 | tf_op jit(solution)/shard_map/all_gather | solution.py:144
  471.6 3.9 select_reduce_fusion
  (99 shorter events, 26.2 us)
Async XLA Ops:
  7.2 80.0 %copy-start = (bf16[1,512,2560]{2,1,0:T(8,128)(2,1)S(1)}, bf16[1,512,2560]{2,1,0:T(8,128)(2,1)}, u32[]{:S(2)}) copy-start(bf16[1,512,2560]{2,1,0:T(8,128)(2,1)} %param.18) | copy-start | bytes 7864324
  7.2 141.8 %all-gather.13.cloned.1.call-start = ((), (), s32[]{:S(2)}) async-start(), calls=%async_computation.3 | async-start | bytes 23158784 | tf_op jit(solution)/shard_map/all_gather | solution.py:63
  7.9 294.7 %all-gather.9.cloned.1.call-start = ((), (), s32[]{:S(2)}) async-start(), calls=%async_computation.1 | async-start | bytes 11796480 | tf_op jit(solution)/shard_map/all_gather | solution.py:20
  174.2 15.5 %copy-start.8 = (f32[4,2816]{1,0:T(4,128)S(1)}, f32[4,2816]{1,0:T(4,128)}, u32[]{:S(2)}) copy-start(f32[4,2816]{1,0:T(4,128)} %param.21) | copy-start | bytes 135172
  174.2 18.2 %copy-start.10 = (f32[2816]{0:T(1024)S(1)}, f32[2816]{0:T(1024)}, u32[]{:S(2)}) copy-start(f32[2816]{0:T(1024)} %param.22) | copy-start | bytes 33796
  185.8 1.6 copy-start.7
  187.4 5.1 %collective-permute-start = (bf16[3,2816]{1,0:T(4,128)(2,1)S(1)}, bf16[3,2816]{1,0:T(4,128)(2,1)S(1)}, u32[]{:S(2)}, u32[]{:S(2)}) collective-permute-start(bf16[3,2816]{1,0:T(4,128)(2,1)S(1)} %slice.59), channel_id=1, source_target_pairs={{0,1},{1,2},{2,3},{3,4},{4,5},{5,6},{6,7},{8,9},{9,10},{10,11},{11... | collective-permute-start | bytes 50696 | tf_op jit(solution)/shard_map/ppermute | solution.py:15
  200.3 1.5 copy-start.5
  211.0 8.2 %copy-start.9 = (f32[40]{0:T(128)S(1)}, f32[40]{0:T(128)}, u32[]{:S(2)}) copy-start(f32[40]{0:T(128)} %param.24) | copy-start | bytes 484
  220.5 5.6 %copy-start.6 = (bf16[2,256,40,64]{1,3,2,0:T(8,128)(2,1)S(1)}, bf16[2,256,40,64]{1,3,2,0:T(8,128)(2,1)}, u32[]{:S(2)}) copy-start(bf16[2,256,40,64]{1,3,2,0:T(8,128)(2,1)} %get-tuple-element.377) | copy-start | bytes 7864324 | tf_op jit(solution)/shard_map/while
  229.0 5.6 %copy-start.6 = (bf16[2,256,40,64]{1,3,2,0:T(8,128)(2,1)S(1)}, bf16[2,256,40,64]{1,3,2,0:T(8,128)(2,1)}, u32[]{:S(2)}) copy-start(bf16[2,256,40,64]{1,3,2,0:T(8,128)(2,1)} %get-tuple-element.377) | copy-start | bytes 7864324 | tf_op jit(solution)/shard_map/while
  238.3 6.8 %copy-start.13 = (u32[256]{0:T(256)S(1)}, u32[256]{0:T(256)}, u32[]{:S(2)}) copy-start(u32[256]{0:T(256)} %constant.93) | copy-start | bytes 3076
  244.0 1.1 copy-start.2
  245.0 136.8 %all-reduce.3.cloned.1.call-start = ((), (), s32[]{:S(2)}) async-start(), calls=%async_computation | async-start | bytes 2621440 | tf_op jit(solution)/shard_map/psum | solution.py:33
  302.8 3.4 copy-start.3
  306.1 77.3 %copy-start.12 = (f32[40]{0:T(128)S(1)}, f32[40]{0:T(128)}, u32[]{:S(2)}) copy-start(f32[40]{0:T(128)} %param.25) | copy-start | bytes 484
  307.4 164.1 %all-gather.11.cloned.1.call-start = ((), (), s32[]{:S(2)}) async-start(), calls=%async_computation.2 | async-start | bytes 5406720 | tf_op jit(solution)/shard_map/all_gather | solution.py:144
  410.6 4.8 %copy-start.4 = (f32[512,2560]{1,0:T(8,128)S(1)}, f32[512,2560]{1,0:T(8,128)}, u32[]{:S(2)}) copy-start(f32[512,2560]{1,0:T(8,128)} %reshape.125) | copy-start | bytes 15728644
  410.6 4.8 %copy-start.11 = (f32[2560]{0:T(1024)S(1)}, f32[2560]{0:T(1024)}, u32[]{:S(2)}) copy-start(f32[2560]{0:T(1024)} %param.26) | copy-start | bytes 30724
  415.4 60.0 %copy-start.1 = (bf16[1,512,2560]{2,1,0:T(8,128)(2,1)S(1)}, bf16[1,512,2560]{2,1,0:T(8,128)(2,1)}, u32[]{:S(2)}) copy-start(bf16[1,512,2560]{2,1,0:T(8,128)(2,1)} %param.18) | copy-start | bytes 7864324
Sparse Core Ops, SparseCore 0:
  11.7 137.2 all-gather.12
  245.2 57.4 all-gather.8
  307.6 74.2 all-reduce.2
  384.9 86.6 all-gather.10
where the time goes:
time: 484 us; the launch traced here: 482 us
  waiting for transfers between devices  235 us (49%)
  blocking collectives  80.5 us (17%)
  local copies, waits for them, and re-layouts  72.7 us (15%)
  other arithmetic  39.5 us (8%)
  matrix products  35.3 us (7%)
  between operations  16 us (3%)
    psum x1, waiting for transfers between devices, broadcast(): return lax.psum(jnp.where(mine, x, jnp.zeros_like(x)), axis)  74.1 us
    all_gather x1, blocking collectives, on_device(): lax.all_gather(step_weight, ('req', 'seq'), axis=0, tiled=True)  70.5 us
    all_gather x1, waiting for transfers between devices, on_device(): lax.all_gather(mix_weight, ('req', 'seq'), axis=0, tiled=True)  60.2 us
    all_gather x1, waiting for transfers between devices, on_device(): piece = lax.all_gather(own_state, 'req', axis=0, tiled=True)  51.5 us
    all_gather x1, waiting for transfers between devices, carried_in(): gathered = jax.tree.map(lambda a: lax.all_gather(a, axis), part)  46 us
    unnamed x30, local copies, waits for them, and re-layouts  32 us
    reshape x2, local copies, waits for them, and re-layouts, on_device(): (inner_out + carried).reshape(span, heads, head_dim)  18.2 us
    dot_general x1, matrix products, on_device(): mixed = jnp.dot(rows, whole_mix, preferred_element_type=jnp.float32)  11.5 us
  transfers between devices with their start and end apart: 5, of which 5 were waited for; matrix products, arithmetic and copies ran while one was open for 10% of the time, Pallas kernels for 0%

commit v1 on v0

v1 whole, which is shorter than its diff:
```python
import functools

import jax
import jax.numpy as jnp
from jax import lax
from jax.experimental import pallas as pl
from jax.experimental.pallas import tpu as pltpu
from jax.sharding import PartitionSpec as P

F32, BF16 = jnp.float32, jnp.bfloat16
MESH = pl.DeviceIdType.MESH
HIGH = lax.Precision.HIGHEST
EPS = 1e-05

SPAN = 512
HALO = 16
CH = 128
NCH = SPAN // CH
D = 2560
SLOTS = 12
GROUPS = 10
LAG = 7
DONE_AT = [(5 * d + 4) // 4 for d in range(8)]


def dot(a, b, **kw):
    return jnp.dot(a, b, preferred_element_type=F32, **kw)


def kernel(
    tok_hbm, wl_ref, cw_ref, hv_ref, len_s, start_s, deal_s,
    res_hbm, fin_ref,
    wb, stage, tokv, valid, conv, out, resv, cum, cum_t, step_t, wk, ec, sc, bt, cc,
    dc, dw, ta, lb, dst, d0, tb, tr, ib, fb, zg, ys, yr, ssq,
    w_send, w_recv, h_sem, tok_sem, g_send, g_recv, sib_send, sib_recv,
    t_send, t_recv, d_send, d_recv, x_send, x_recv, i_send, i_recv,
    f_send, f_recv, z_send, z_recv, y_send, y_recv, o_sem,
):
    r, q = lax.axis_index("req"), lax.axis_index("seq")
    z, y, x, c = r // 4, r % 4, q // 2, q % 2
    yn = [(z * 4 + (y + d) % 4, q) for d in range(4)]
    zn = [(((z + d) % 8) * 4 + y, q) for d in range(8)]
    qn = [(r, (q + d) % 8) for d in range(8)]
    yp, ym, zp, zm = yn[1], yn[3], zn[1], zn[7]
    sib = (r, q + 1 - 2 * c)
    yi = [(y + d) % 4 for d in range(4)]
    zi = [(z + d) % 8 for d in range(8)]

    def remote(src, to, ssem, rsem, dev):
        return pltpu.make_async_remote_copy(
            src_ref=src, dst_ref=to, send_sem=ssem, recv_sem=rsem,
            device_id=dev, device_id_type=MESH,
        )

    barrier = pltpu.get_barrier_semaphore()
    partners = qn[1:] + yn[1:] + [zp, zm]
    for dev in partners:
        pl.semaphore_signal(barrier, inc=1, device_id=dev, device_id_type=MESH)
    tok_copy = pltpu.make_async_copy(tok_hbm, tokv.at[pl.ds(HALO, SPAN)], tok_sem)
    tok_copy.start()
    pl.semaphore_wait(barrier, len(partners))

    own_w = pltpu.make_async_copy(wl_ref.at[c], stage.at[q], w_recv.at[7])
    own_w.start()
    w_copies = []
    for d in range(1, 8):
        to = (q + d) % 8
        w_copies.append(
            remote(wl_ref.at[to % 2], stage.at[q], w_send.at[d - 1], w_recv.at[d - 1], qn[d])
        )
        w_copies[-1].start()
    halo = remote(
        tok_hbm.at[pl.ds(SPAN - HALO, HALO)], tokv.at[pl.ds(0, HALO)],
        h_sem.at[0], h_sem.at[1], qn[1],
    )
    halo.start()

    request = deal_s[r]
    first = start_s[request]
    last = first + len_s[request]
    place = lax.broadcasted_iota(jnp.int32, (SPAN + HALO, 128), 0) + (q * SPAN - HALO)
    valid[...] = jnp.where((place >= first) & (place < last), 1.0, 0.0)
    ssq[...] = jnp.zeros_like(ssq)

    own_w.wait()
    for d in range(1, 8):
        src = (q - d) % 8
        remote(
            wl_ref.at[0], stage.at[src], w_send.at[d - 1], w_recv.at[d - 1], qn[d]
        ).wait_recv()
    row = lax.broadcasted_iota(jnp.int32, (80, 128), 0)
    col = lax.broadcasted_iota(jnp.int32, (80, 128), 1)
    pick = jnp.where(col == (row // 10) * 16 + row % 10, 1.0, 0.0).astype(BF16)
    for s in range(SLOTS):
        part = stage[:, :, s * 128 : (s + 1) * 128].reshape(128, 128)
        wb[c, s, z, y] = dot(pick, part).astype(BF16)
    for copy in w_copies:
        copy.wait_send()
    tok_copy.wait()
    halo.wait_send()
    halo.wait_recv()

    def blk(s, dz, dy):
        return wb.at[c, s, zi[dz], yi[dy]]

    def lo(ref):
        return ref.at[pl.ds(0, 48)]

    def hi(ref):
        return ref.at[pl.ds(48, 32)]

    def zset(s, dz):
        return wb.at[0, s, zi[dz]]

    def yset(s, dy):
        return wb.at[1, s, :, yi[dy]]

    def messages(core, s):
        if core == 0:
            return [
                (blk(s, 0, 3), blk(s, 0, 0), yp),
                (blk(s, 0, 1), blk(s, 0, 0), ym),
                (lo(blk(s, 0, 2)), lo(blk(s, 0, 3)), yp),
                (hi(blk(s, 0, 2)), hi(blk(s, 0, 1)), ym),
                (zset(s, 7), zset(s, 0), zp),
                (zset(s, 1), zset(s, 0), zm),
                (zset(s, 6), zset(s, 7), zp),
                (zset(s, 2), zset(s, 1), zm),
                (zset(s, 5), zset(s, 6), zp),
                (zset(s, 3), zset(s, 2), zm),
                (zset(s, 4).at[pl.ds(0, 2)], zset(s, 5).at[pl.ds(0, 2)], zp),
                (zset(s, 4).at[pl.ds(2, 2)], zset(s, 3).at[pl.ds(2, 2)], zm),
            ]
        return [
            (blk(s, 7, 0), blk(s, 0, 0), zp),
            (blk(s, 1, 0), blk(s, 0, 0), zm),
            (blk(s, 6, 0), blk(s, 7, 0), zp),
            (blk(s, 2, 0), blk(s, 1, 0), zm),
            (blk(s, 5, 0), blk(s, 6, 0), zp),
            (blk(s, 3, 0), blk(s, 2, 0), zm),
            (lo(blk(s, 4, 0)), lo(blk(s, 5, 0)), zp),
            (hi(blk(s, 4, 0)), hi(blk(s, 3, 0)), zm),
            (yset(s, 3), yset(s, 0), yp),
            (yset(s, 1), yset(s, 0), ym),
            (wb.at[1, s, pl.ds(0, 4), yi[2]], wb.at[1, s, pl.ds(0, 4), yi[3]], yp),
            (wb.at[1, s, pl.ds(4, 4), yi[2]], wb.at[1, s, pl.ds(4, 4), yi[1]], ym),
        ]

    def send(core, s, m):
        _, src, dev = messages(core, s)[m]
        remote(src, src, g_send.at[s, m], g_recv.at[s, m], dev).start()

    def got(core, s, m):
        here, _, dev = messages(core, s)[m]
        remote(here, here, g_send.at[s, m], g_recv.at[s, m], dev).wait_recv()

    def sent(core, s, m):
        _, src, dev = messages(core, s)[m]
        remote(src, src, g_send.at[s, m], g_recv.at[s, m], dev).wait_send()

    def ring_stage(core, s, k):
        if k > 0:
            got(core, s, 2 * k - 2)
            got(core, s, 2 * k - 1)
        if k < 6:
            send(core, s, 2 * k)
            send(core, s, 2 * k + 1)
        else:
            half = wb.at[core, s]
            remote(half, half, sib_send.at[s], sib_recv.at[s], sib).start()

    def has(core, s):
        return (s != 1) if core == 0 else True

    def expander(g, rows, kind):
        i = lax.broadcasted_iota(jnp.int32, (rows, 256), 0)
        j = lax.broadcasted_iota(jnp.int32, (rows, 256), 1)
        return jnp.where((i & 127) == 4 * g + (j >> 6), 1.0, 0.0).astype(kind)

    def project(w):
        mixed = dot(tokv[...], w)
        v = valid[...]
        for half in range(2):
            part = mixed[:, half * 128 : half * 128 + 128] * v
            conv[half] = part.astype(BF16).astype(F32)

    def convolve(half, j, index):
        lanes = slice(half * 128, half * 128 + 128)
        acc = jnp.broadcast_to(cw_ref[index, 4:5, lanes], (CH, 128))
        for k in range(4):
            acc = acc + cw_ref[index, k : k + 1, lanes] * conv[half, pl.ds(13 + k + CH * j, CH), :]
        return (0.5 * acc * (1.0 + jnp.tanh(0.5 * acc))).astype(BF16)

    def halves(v):
        top = v.astype(BF16)
        low = (v - top.astype(F32)).astype(BF16)
        return top, low

    ri = lax.broadcasted_iota(jnp.int32, (CH, CH), 0)
    ci = lax.broadcasted_iota(jnp.int32, (CH, CH), 1)

    def prepare():
        raw = dot(tokv[pl.ds(HALO, SPAN), :], wb[1, 0].reshape(D, 128))
        project(jnp.concatenate([wb[0, 0].reshape(D, 128), wb[1, 1].reshape(D, 128)], axis=1))
        tri = jnp.where(ri >= ci, 1.0, 0.0)
        before = jnp.zeros((1, 128), F32)
        for j in range(NCH):
            rows = slice(j * CH, (j + 1) * CH)
            b = convolve(0, j, 0)
            cj = convolve(1, j, 0)
            cc[j] = jnp.concatenate([cj, cj], axis=1)
            bt[j] = b.astype(F32).T.astype(BF16)
            score = lax.dot_general(cj, b, (((1,), (1,)), ((), ())), preferred_element_type=F32)
            sc[j] = jnp.where(ri >= ci, score, 0.0)
            v = raw[rows] + hv_ref[0:1, :]
            step = jnp.maximum(v, 0.0) + jnp.log1p(jnp.exp(-jnp.abs(v)))
            step = step * valid[pl.ds(HALO + j * CH, CH), :]
            total = dot(tri, -step * hv_ref[1:2, :], precision=HIGH)
            cum[pl.ds(j * CH, CH), :] = total
            cum_t[j] = total.T
            step_t[j] = step.T
            end = total[CH - 1 : CH, :]
            top, low = halves(jnp.exp(end - total) * step)
            wk[pl.ds(j * CH, CH), :] = jnp.concatenate([top, low], axis=1)
            top, low = halves(jnp.exp(total))
            ec[pl.ds(j * CH, CH), :] = jnp.concatenate([top, low], axis=1)
            dc[j : j + 1, :] = jnp.exp(end)
            dc[4 + j : 5 + j, :] = jnp.exp(before)
            before = before + end
        ta[q] = jnp.broadcast_to(before, (8, 128))
        for d in range(1, 8):
            remote(ta.at[q], ta.at[q], t_send.at[d - 1], t_recv.at[d - 1], qn[d]).start()

    def link_decays():
        for d in range(1, 8):
            src = (q - d) % 8
            remote(ta.at[src], ta.at[src], t_send.at[d - 1], t_recv.at[d - 1], qn[d]).wait_recv()
        tot = [ta[d][0:1, :] for d in range(8)]
        dw[...] = jnp.zeros_like(dw)
        for xs in range(3):
            acc = jnp.zeros((1, 128), F32)
            for d in range(2 * xs + 2, 8):
                acc = acc + tot[d] * jnp.where(d < 2 * x, 1.0, 0.0)
            dw[xs : xs + 1, :] = jnp.exp(acc)
        dw[3:4, :] = jnp.exp(ta[2 * x][0:1, :])
        dw[4:5, :] = jnp.exp(ta[2 * x + 1][0:1, :])

    lane = lax.broadcasted_iota(jnp.int32, (CH, 128), 1)

    def group(g):
        s = g + 2
        project(jnp.concatenate([wb[0, s].reshape(D, 128), wb[1, s].reshape(D, 128)], axis=1))
        spread = expander(g, 256, BF16)
        decays = dot(dc[...], expander(g, 128, F32), precision=HIGH)
        cums = cum[...]
        for j in range(NCH):
            xj = [convolve(half, j, g + 1) for half in range(2)]
            weight = dot(wk[pl.ds(j * CH, CH), :], spread)
            xf = jnp.concatenate(xj, axis=1).astype(F32)
            local = dot(bt[j], (weight * xf).astype(BF16))
            if j > 0:
                local = local + decays[j : j + 1, :] * lb[g, j - 1]
            if j < NCH - 1:
                lb[g, j] = local
            else:
                dst[g] = local
            for half in range(2):
                mix = []
                for e in range(2):
                    h = 2 * half + e
                    cq = jnp.broadcast_to(cums[j * CH : (j + 1) * CH, h : h + 1], (CH, CH))
                    ck = cum_t[j, pl.ds(4 * g + h, 1), :]
                    sk = step_t[j, pl.ds(4 * g + h, 1), :]
                    mix.append((jnp.exp(jnp.minimum(cq - ck, 0.0)) * sc[j] * sk).astype(BF16))
                zero = jnp.zeros_like(xj[half])
                pair = jnp.concatenate(
                    [jnp.where(lane < 64, xj[half], zero), jnp.where(lane < 64, zero, xj[half])],
                    axis=0,
                )
                inner = dot(jnp.concatenate(mix, axis=1), pair)
                lanes = slice(half * 128, half * 128 + 128)
                skip = cw_ref[g + 1, 5:6, lanes]
                out[g, pl.ds(j * CH, CH), lanes] = inner + skip * xj[half].astype(F32)
        cum[...] = pltpu.roll(cums, 124, 1)

        @pl.when(c == 0)
        def _():
            remote(dst.at[g], d0.at[g], d_send.at[g], d_recv.at[g], sib).start()

    def chip_total(g):
        @pl.when(c == 1)
        def _():
            remote(dst.at[g], d0.at[g], d_send.at[g], d_recv.at[g], sib).wait_recv()
            decays = dot(dw[...], expander(g, 128, F32), precision=HIGH)
            tb[g] = (decays[4:5, :] * d0[g] + dst[g]).astype(BF16)
            for dx in range(1, 4):
                @pl.when(x + dx < 4)
                def _():
                    remote(
                        tb.at[g], tr.at[dx - 1, g], x_send.at[dx - 1, g], x_recv.at[dx - 1, g],
                        qn[2 * dx],
                    ).start()

    def chip_entry(g):
        @pl.when(c == 1)
        def _():
            decays = dot(dw[...], expander(g, 128, F32), precision=HIGH)
            ib[g] = jnp.zeros((128, 256), F32)
            for dx in range(1, 4):
                for xs in range(4 - dx):
                    @pl.when(x == xs + dx)
                    def _():
                        remote(
                            tb.at[g], tr.at[dx - 1, g], x_send.at[dx - 1, g],
                            x_recv.at[dx - 1, g], qn[2 * dx],
                        ).wait_recv()
                        ib[g] += decays[xs : xs + 1, :] * tr[dx - 1, g].astype(F32)
            remote(ib.at[g], ib.at[g], i_send.at[g], i_recv.at[g], sib).start()

    def late(g):
        spread = expander(g, 256, BF16)
        small = expander(g, 128, F32)
        inner = dot(dc[...], small, precision=HIGH)
        outer = dot(dw[...], small, precision=HIGH)

        @pl.when(c == 0)
        def _():
            remote(ib.at[g], ib.at[g], i_send.at[g], i_recv.at[g], sib).wait_recv()
            d0[g] = ib[g]

        @pl.when(c == 1)
        def _():
            d0[g] = d0[g] + outer[3:4, :] * ib[g]

        incoming = d0[g]
        for j in range(NCH):
            entry = inner[4 + j : 5 + j, :] * incoming
            if j > 0:
                entry = entry + lb[g, j - 1]
            carried = dot(cc[j], jnp.concatenate(halves(entry), axis=0))
            carried = carried * dot(ec[pl.ds(j * CH, CH), :], spread)
            full = out[g, pl.ds(j * CH, CH), :] + carried
            out[g, pl.ds(j * CH, CH), :] = full
            square = full * full
            ssq[pl.ds(j * CH, CH), :] += square[:, :128] + square[:, 128:]

        @pl.when(q == 7)
        def _():
            leaving = outer[4:5, :] * incoming + dst[g]
            fb[pl.ds(4 * g, 4)] = leaving.T.reshape(4, 64, 128).astype(BF16)
            for dest in range(7):
                @pl.when(g == DONE_AT[dest])
                def _():
                    remote(
                        fb.at[pl.ds(5 * dest, 5)], zg.at[z], f_send.at[dest], f_recv, (r, dest)
                    ).start()

    def body(t, carry):
        for k in range(7):
            s = t - k
            @pl.when((s >= 0) & (s < SLOTS))
            def _():
                @pl.when((c == 0) & has(0, s))
                def _():
                    ring_stage(0, s, k)

                @pl.when(c == 1)
                def _():
                    ring_stage(1, s, k)
        s = t - LAG
        @pl.when((s >= 0) & (s < SLOTS))
        def _():
            @pl.when(c == 0)
            def _():
                half = wb.at[1, s]
                remote(half, half, sib_send.at[s], sib_recv.at[s], sib).wait_recv()

            @pl.when((c == 1) & has(0, s))
            def _():
                half = wb.at[0, s]
                remote(half, half, sib_send.at[s], sib_recv.at[s], sib).wait_recv()

        g = s - 2

        @pl.when(g == -1)
        def _():
            prepare()

        @pl.when((g >= 0) & (g < GROUPS))
        def _():
            group(g)

        @pl.when(g == 0)
        def _():
            link_decays()

        @pl.when((g >= 1) & (g < GROUPS + 1))
        def _():
            chip_total(g - 1)

        @pl.when((g >= 2) & (g < GROUPS + 2))
        def _():
            chip_entry(g - 2)

        @pl.when((g >= 3) & (g < GROUPS + 3))
        def _():
            late(g - 3)

        return carry

    lax.fori_loop(0, LAG + SLOTS + 3, body, 0)

    def zroute(m):
        heads = [pl.ds(0, 5)] * 6 + [pl.ds(0, 3), pl.ds(3, 2)]
        dz = [0, 0, 7, 1, 6, 2, 5, 3][m]
        here = [7, 1, 6, 2, 5, 3, 4, 4][m]
        src = zg.at[zi[dz], heads[m]]
        to = zg.at[zi[here], heads[m]]
        dev = zp if m % 2 == 0 else zm
        return (
            remote(src, src, z_send.at[m], z_recv.at[m], dev),
            remote(to, to, z_send.at[m], z_recv.at[m], dev),
        )

    @pl.when(q == 7)
    def _():
        zg[z] = fb[35:40]

    @pl.when(q != 7)
    def _():
        remote(fb.at[pl.ds(0, 5)], zg.at[z], f_send.at[0], f_recv, (r, 0)).wait_recv()

    zroute(0)[0].start()
    zroute(1)[0].start()

    o_copies = []

    def normed(j):
        rows = pl.ds(j * CH, CH)
        mean = jnp.sum(ssq[rows, :], axis=1, keepdims=True) * (1.0 / D)
        factor = lax.rsqrt(mean + EPS) * valid[pl.ds(HALO + j * CH, CH), :][:, 0:1]
        for g in range(GROUPS):
            gain = cw_ref[g + 1, 6:7, :]
            resv[rows, 256 * g : 256 * g + 256] = (out[g, rows, :] * factor * gain).astype(BF16)
        copy = pltpu.make_async_copy(resv.at[rows], res_hbm.at[rows], o_sem.at[j])
        copy.start()
        o_copies.append(copy)

    for k in range(3):
        normed(k)
        for e in range(2):
            zroute(2 * k + e)[1].wait_recv()
            zroute(2 * k + 2 + e)[0].start()
    normed(3)
    for e in range(2):
        zroute(6 + e)[1].wait_recv()

    def holder(dy):
        target = z * 4 + yi[dy]

        def look(s, found):
            return jnp.where(deal_s[s] == target, s, found)

        return lax.fori_loop(0, 32, look, 0)

    y_copies = []
    for dy in range(1, 4):
        ys[dy - 1] = zg[holder(dy) // 4]
        copy = remote(ys.at[dy - 1], yr.at[dy], y_send.at[dy - 1], y_recv.at[dy - 1], yn[dy])
        copy.start()
        y_copies.append(copy)
    mine = holder(0)
    yr[0] = zg[mine // 4]
    for copy in y_copies:
        copy.wait_recv()
    fin_ref[...] = yr[(y + 4 - mine % 4) % 4].astype(F32)

    for copy in y_copies:
        copy.wait_send()
    for m in range(8):
        zroute(m)[0].wait_send()
    for copy in o_copies:
        copy.wait()
    for d in range(1, 8):
        remote(ta.at[q], ta.at[q], t_send.at[d - 1], t_recv.at[d - 1], qn[d]).wait_send()

    def drain_slot(s, carry):
        for core in range(2):
            @pl.when((c == core) & has(core, s))
            def _():
                for m in range(12):
                    sent(core, s, m)
                half = wb.at[core, s]
                remote(half, half, sib_send.at[s], sib_recv.at[s], sib).wait_send()
        return carry

    lax.fori_loop(0, SLOTS, drain_slot, 0)

    def drain_group(g, carry):
        @pl.when(c == 0)
        def _():
            remote(dst.at[g], d0.at[g], d_send.at[g], d_recv.at[g], sib).wait_send()

        @pl.when(c == 1)
        def _():
            remote(ib.at[g], ib.at[g], i_send.at[g], i_recv.at[g], sib).wait_send()
            for dx in range(1, 4):
                @pl.when(x + dx < 4)
                def _():
                    remote(
                        tb.at[g], tr.at[dx - 1, g], x_send.at[dx - 1, g], x_recv.at[dx - 1, g],
                        qn[2 * dx],
                    ).wait_send()
        return carry

    lax.fori_loop(0, GROUPS, drain_group, 0)

    @pl.when(q == 7)
    def _():
        for dest in range(7):
            remote(
                fb.at[pl.ds(5 * dest, 5)], zg.at[z], f_send.at[dest], f_recv, (r, dest)
            ).wait_send()


def on_device(
    tokens, mix_weight, step_weight, conv_weight, conv_bias, step_bias, decay_rate,
    skip_gain, norm_gain, prompt_len, prompt_start, deal,
):
    heads = decay_rate.shape[0]
    tiles = mix_weight.reshape(10, 22, 128)
    step_tile = jnp.pad(step_weight, ((0, 0), (0, 128 - heads)))[:, None]
    even = jnp.concatenate([tiles[:, 20:21], jnp.zeros_like(step_tile), tiles[:, 0:20:2]], axis=1)
    odd = jnp.concatenate([step_tile, tiles[:, 21:22], tiles[:, 1:20:2]], axis=1)
    wl = jnp.pad(jnp.stack([even, odd]).reshape(2, 10, 1536), ((0, 0), (0, 6), (0, 0)))
    per_head = 2560 // heads
    extra = jnp.stack([conv_bias[:2560], jnp.repeat(skip_gain, per_head), norm_gain,
                       jnp.zeros_like(norm_gain)])
    cw_x = jnp.concatenate([conv_weight[:, :2560], extra]).reshape(8, GROUPS, 256)
    cw_bc = jnp.pad(
        jnp.concatenate([conv_weight[:, 2560:], conv_bias[None, 2560:]]), ((0, 3), (0, 0))
    )
    cw = jnp.concatenate([cw_bc[:, None], cw_x], axis=1).transpose(1, 0, 2)
    hv = jnp.pad(jnp.stack([step_bias, decay_rate]), ((0, 6), (0, 128 - heads)))

    vm, dma = pltpu.VMEM, pltpu.SemaphoreType.DMA
    vspec = pl.BlockSpec(memory_space=pltpu.VMEM)
    sspec = pl.BlockSpec(memory_space=pltpu.SMEM)
    aspec = pl.BlockSpec(memory_space=pl.ANY)
    result, final = pl.pallas_call(
        kernel,
        out_shape=(
            jax.ShapeDtypeStruct((SPAN, D), BF16),
            jax.ShapeDtypeStruct((5, 64, 128), F32),
        ),
        in_specs=[aspec, vspec, vspec, vspec, sspec, sspec, sspec],
        out_specs=(aspec, vspec),
        scratch_shapes=[
            vm((2, SLOTS, 8, 4, 80, 128), BF16),
            vm((8, 16, 1536), BF16),
            vm((SPAN + HALO, D), BF16),
            vm((SPAN + HALO, 128), F32),
            vm((2, SPAN + HALO, 128), F32),
            vm((GROUPS, SPAN, 256), F32),
            vm((SPAN, D), BF16),
            vm((SPAN, 128), F32),
            vm((NCH, 128, CH), F32),
            vm((NCH, 128, CH), F32),
            vm((SPAN, 256), BF16),
            vm((SPAN, 256), BF16),
            vm((NCH, CH, CH), F32),
            vm((NCH, 128, CH), BF16),
            vm((NCH, CH, 256), BF16),
            vm((8, 128), F32),
            vm((8, 128), F32),
            vm((8, 8, 128), F32),
            vm((GROUPS, 3, 128, 256), F32),
            vm((GROUPS, 128, 256), F32),
            vm((GROUPS, 128, 256), F32),
            vm((GROUPS, 128, 256), BF16),
            vm((3, GROUPS, 128, 256), BF16),
            vm((GROUPS, 128, 256), F32),
            vm((40, 64, 128), BF16),
            vm((8, 5, 64, 128), BF16),
            vm((3, 5, 64, 128), BF16),
            vm((4, 5, 64, 128), BF16),
            vm((SPAN, 128), F32),
            dma((7,)), dma((8,)), dma((2,)), dma,
            dma((SLOTS, 12)), dma((SLOTS, 12)), dma((SLOTS,)), dma((SLOTS,)),
            dma((7,)), dma((7,)), dma((GROUPS,)), dma((GROUPS,)),
            dma((3, GROUPS)), dma((3, GROUPS)), dma((GROUPS,)), dma((GROUPS,)),
            dma((7,)), dma, dma((8,)), dma((8,)), dma((3,)), dma((3,)), dma((NCH,)),
        ],
        compiler_params=pltpu.CompilerParams(
            collective_id=0, has_side_effects=True, vmem_limit_bytes=62 * 1024 * 1024
        ),
    )(tokens[0], wl, cw, hv, prompt_len, prompt_start, deal)
    return (result[None], final[None])


def solution(mesh):
    return jax.shard_map(
        on_device,
        mesh=mesh,
        in_specs=(P("req", "seq", None), P(("req", "seq"), None), P(("req", "seq"), None))
        + (P(),) * 9,
        out_specs=(P("req", "seq", None), P("req", "seq", None, None)),
        check_vma=False,
    )
```

time: 484 us -> 135 us (0.28)
  waiting for transfers between devices: 235 us -> 0 us
  Pallas kernels: 0 us -> 120 us
  blocking collectives: 80.5 us -> 0 us
  local copies, waits for them, and re-layouts: 72.7 us -> 10.6 us
  other arithmetic: 39.5 us -> 2.67 us
  matrix products: 35.3 us -> 0 us
  between operations: 16 us -> 0.7 us
    all_gather x3 -> x0, waiting for transfers between devices: 158 us -> none  [the longest x1 60.2 us: on_device(): lax.all_gather(mix_weight, ('req', 'seq'), axis=0, tiled=True)]
    pallas_call x0 -> x1, Pallas kernels: none -> 120 us  [on_device(): pl.pallas_call(kernel, out_shape=(jax.ShapeDtypeStruct((SPAN, D), BF16),...]
    psum x1 -> x0, waiting for transfers between devices: 74.1 us -> none  [broadcast(): return lax.psum(jnp.where(mine, x, jnp.zeros_like(x)), axis)]
    all_gather x1 -> x0, blocking collectives: 70.5 us -> none  [on_device(): lax.all_gather(step_weight, ('req', 'seq'), axis=0, tiled=True)]
    dot_general x9 -> x0, matrix products: 35.3 us -> none  [the longest x1 11.5 us: on_device(): mixed = jnp.dot(rows, whole_mix, preferred_element_type=jnp.float32)]
    unnamed x30 -> x4, local copies, waits for them, and re-layouts: 32 us -> 4.11 us
    reshape x3 -> x1, local copies, waits for them, and re-layouts: 18.3 us -> 0.96 us  [on_device(): tiles = mix_weight.reshape(10, 22, 128)]
    reduce_sum x6 -> x0, other arithmetic: 13.7 us -> none  [the longest x1 4.42 us: on_device(): factor = lax.rsqrt(jnp.mean(flat * flat, axis=1, keepdims=True) + EPS)]
  transfers between devices with their start and end apart: 5 -> 0, of which waited for: 5 -> 0; matrix products, arithmetic and copies ran while one was open for 10% -> 0% of each run, Pallas kernels for 0% -> 0%
where the time goes in v1:
time: 135 us; the launch traced here: 134 us
  Pallas kernels  120 us (89%)
  local copies, waits for them, and re-layouts  10.6 us (8%)
  other arithmetic  2.67 us (2%)
    pallas_call x1, Pallas kernels, on_device(): pl.pallas_call(kernel, out_shape=(jax.ShapeDtypeStruct((SPAN, D), BF16),...  120 us
    unnamed x4, local copies, waits for them, and re-layouts  4.11 us

profile of v1, /device:TPU:2, one launch (start us, length us, event | category | flops | bytes accessed | tf_op | source)
XLA Modules:
  0.0 133.6 jit_solution(6053972454045082487)
XLA Ops:
  0.6 0.1 pad.32.clone
  0.7 0.7 slice.29
  1.4 0.7 pad_bitcast_fusion
  2.1 1.3 select_maximum_fusion.1.hv_ref
  3.4 0.7 slice.28
  4.1 0.7 broadcast_in_dim.29
  4.8 0.7 concatenate.28
  5.5 0.7 concatenate.27
  6.2 0.1 broadcast_in_dim.30
  6.3 0.1 broadcast_in_dim.31
  6.4 0.8 slice.30
  7.2 0.1 concatenate.29
  7.3 0.6 maximum_bitcast_fusion.cw_ref
  7.9 1.0 reshape.28
  9.0 0.1 pad_maximum_fusion
  9.2 0.7 fusion.2.wl_ref
  9.9 119.6 %shard_map.131 = (bf16[512,2560]{1,0:T(8,128)(2,1)}, f32[5,64,128]{2,1,0:T(8,128)}) custom-call(bf16[512,2560]{1,0:T(8,128)(2,1)} %bitcast.15, bf16[2,16,1536]{2,1,0:T(8,128)(2,1)} %fusion.2.wl_ref, f32[11,8,256]{2,1,0:T(8,128)} %maximum_bitcast_fusion.cw_ref, f32[8,128]{1,0:T(8,128)} %select_maximum_fusion.1.hv_ref, s32[32]{0:T(128)} %len_s.1, s32[32]{0:T(128)} %start_s.1, ...), custom_call_target="tpu_custom_call" | custom-call | tf_op jit(solution)/shard_map/pallas_call | solution.py:550
  129.5 0.0 copy-start
  129.5 3.4 %copy.18 = bf16[1,512,2560]{2,1,0:T(8,128)(2,1)} copy(bf16[1,512,2560]{2,1,0:T(8,128)(2,1)} %bitcast.16) | data formatting | bytes 5242880
  132.9 0.0 copy-done
  132.9 0.7 copy.19
  (8 shorter events, 0.2 us)
Async XLA Ops:
  129.5 3.5 %copy-start = (f32[5,64,128]{2,1,0:T(8,128)S(1)}, f32[5,64,128]{2,1,0:T(8,128)}, u32[]{:S(2)}) copy-start(f32[5,64,128]{2,1,0:T(8,128)} %get-tuple-element.5) | copy-start | bytes 491524

commit v2 on v1

v2 whole, which is shorter than its diff:
```python
import functools

import jax
import jax.numpy as jnp
from jax import lax
from jax.experimental import pallas as pl
from jax.experimental.pallas import tpu as pltpu
from jax.sharding import PartitionSpec as P

F32, BF16 = jnp.float32, jnp.bfloat16
MESH = pl.DeviceIdType.MESH
HIGH = lax.Precision.HIGHEST
EPS = 1e-05

SPAN = 512
HALO = 16
CH = 128
NCH = SPAN // CH
D = 2560
SLOTS = 12
GROUPS = 10
GAP = 2
LAG = 6 * GAP + 1
LOG2E = 1.4426950408889634
TO_TOTAL, TO_ENTRY, TO_LATE = 1, 3, 5


def dot(a, b, **kw):
    return jnp.dot(a, b, preferred_element_type=F32, **kw)


def kernel(
    tok_hbm, mix_ref, sw_ref, cw_ref, vec_ref, len_s, start_s, deal_s,
    res_hbm, fin_ref,
    wb, wl_ref, stage, tokv, valid, conv, hold, out, resv, cum, cum_t, wk, ec, sc, bt, cc,
    dcw, dx, ta, lb, dst, d0, tb, tr, ib, fd, zg, ys, yr, ssq,
    w_send, w_recv, h_sem, tok_sem, g_send, g_recv, sib_send, sib_recv,
    t_send, t_recv, d_send, d_recv, x_send, x_recv, i_send, i_recv,
    f_send, f_recv, z_send, z_recv, y_send, y_recv, o_sem,
):
    r, q = lax.axis_index("req"), lax.axis_index("seq")
    z, y, x, c = r // 4, r % 4, q // 2, q % 2
    yn = [(z * 4 + (y + d) % 4, q) for d in range(4)]
    zn = [(((z + d) % 8) * 4 + y, q) for d in range(8)]
    qn = [(r, (q + d) % 8) for d in range(8)]
    yp, ym, zp, zm = yn[1], yn[3], zn[1], zn[7]
    sib = (r, q + 1 - 2 * c)
    yi = [(y + d) % 4 for d in range(4)]
    zi = [(z + d) % 8 for d in range(8)]

    def remote(src, to, ssem, rsem, dev):
        return pltpu.make_async_remote_copy(
            src_ref=src, dst_ref=to, send_sem=ssem, recv_sem=rsem,
            device_id=dev, device_id_type=MESH,
        )

    barrier = pltpu.get_barrier_semaphore()
    partners = qn[1:] + yn[1:] + [zp, zm]
    for dev in partners:
        pl.semaphore_signal(barrier, inc=1, device_id=dev, device_id_type=MESH)
    tok_copy = pltpu.make_async_copy(tok_hbm, tokv.at[pl.ds(HALO, SPAN)], tok_sem)
    tok_copy.start()
    wl_ref[...] = jnp.zeros_like(wl_ref)
    wl_ref[0, 0:10, 0:40] = sw_ref[...]
    wl_ref[0, 0:10, 256:1536] = mix_ref[:, 0:1280]
    wl_ref[1, 0:10, 0:256] = mix_ref[:, 2560:2816]
    wl_ref[1, 0:10, 256:1536] = mix_ref[:, 1280:2560]
    pl.semaphore_wait(barrier, len(partners))

    waves = [pl.ds(0, 256), pl.ds(256, 1280)]
    w_copies = []
    for n, cols in enumerate(waves):
        own_w = pltpu.make_async_copy(wl_ref.at[c, :, cols], stage.at[q, :, cols], w_recv.at[n, 7])
        own_w.start()
        w_copies.append([own_w])
        for d in range(1, 8):
            to = (q + d) % 8
            copy = remote(
                wl_ref.at[to % 2, :, cols], stage.at[q, :, cols],
                w_send.at[n, d - 1], w_recv.at[n, d - 1], qn[d],
            )
            copy.start()
            w_copies[n].append(copy)
    halo = remote(
        tok_hbm.at[pl.ds(SPAN - HALO, HALO)], tokv.at[pl.ds(0, HALO)],
        h_sem.at[0], h_sem.at[1], qn[1],
    )
    halo.start()

    def holder(dy):
        target = z * 4 + yi[dy]

        def look(s, found):
            return jnp.where(deal_s[s] == target, s, found)

        return lax.fori_loop(0, 32, look, 0)

    for dy in range(4):
        hold[dy] = holder(dy)
    request = deal_s[r]
    first = start_s[request]
    last = first + len_s[request]
    place = lax.broadcasted_iota(jnp.int32, (SPAN + HALO, 128), 0) + (q * SPAN - HALO)
    valid[...] = jnp.where((place >= first) & (place < last), 1.0, 0.0)
    ssq[...] = jnp.zeros_like(ssq)

    row = lax.broadcasted_iota(jnp.int32, (80, 128), 0)
    col = lax.broadcasted_iota(jnp.int32, (80, 128), 1)
    pick = jnp.where(col == (row // 10) * 16 + row % 10, 1.0, 0.0).astype(BF16)

    def assemble(n, slots):
        w_copies[n][0].wait()
        for d in range(1, 8):
            to = stage.at[(q - d) % 8, :, waves[n]]
            remote(to, to, w_send.at[n, d - 1], w_recv.at[n, d - 1], qn[d]).wait_recv()
        for s in slots:
            part = stage[:, :, s * 128 : (s + 1) * 128].reshape(128, 128)
            wb[c, s, z, y] = dot(pick, part).astype(BF16)

    def blk(s, dz, dy):
        return wb.at[c, s, zi[dz], yi[dy]]

    def lo(ref):
        return ref.at[pl.ds(0, 48)]

    def hi(ref):
        return ref.at[pl.ds(48, 32)]

    def zset(s, dz):
        return wb.at[0, s, zi[dz]]

    def yset(s, dy):
        return wb.at[1, s, :, yi[dy]]

    def messages(core, s):
        if core == 0:
            return [
                (blk(s, 0, 3), blk(s, 0, 0), yp),
                (blk(s, 0, 1), blk(s, 0, 0), ym),
                (lo(blk(s, 0, 2)), lo(blk(s, 0, 3)), yp),
                (hi(blk(s, 0, 2)), hi(blk(s, 0, 1)), ym),
                (zset(s, 7), zset(s, 0), zp),
                (zset(s, 1), zset(s, 0), zm),
                (zset(s, 6), zset(s, 7), zp),
                (zset(s, 2), zset(s, 1), zm),
                (zset(s, 5), zset(s, 6), zp),
                (zset(s, 3), zset(s, 2), zm),
                (zset(s, 4).at[pl.ds(0, 2)], zset(s, 5).at[pl.ds(0, 2)], zp),
                (zset(s, 4).at[pl.ds(2, 2)], zset(s, 3).at[pl.ds(2, 2)], zm),
            ]
        return [
            (blk(s, 7, 0), blk(s, 0, 0), zp),
            (blk(s, 1, 0), blk(s, 0, 0), zm),
            (blk(s, 6, 0), blk(s, 7, 0), zp),
            (blk(s, 2, 0), blk(s, 1, 0), zm),
            (blk(s, 5, 0), blk(s, 6, 0), zp),
            (blk(s, 3, 0), blk(s, 2, 0), zm),
            (lo(blk(s, 4, 0)), lo(blk(s, 5, 0)), zp),
            (hi(blk(s, 4, 0)), hi(blk(s, 3, 0)), zm),
            (yset(s, 3), yset(s, 0), yp),
            (yset(s, 1), yset(s, 0), ym),
            (wb.at[1, s, pl.ds(0, 4), yi[2]], wb.at[1, s, pl.ds(0, 4), yi[3]], yp),
            (wb.at[1, s, pl.ds(4, 4), yi[2]], wb.at[1, s, pl.ds(4, 4), yi[1]], ym),
        ]

    def send(core, s, m):
        _, src, dev = messages(core, s)[m]
        remote(src, src, g_send.at[s, m], g_recv.at[s, m], dev).start()

    def got(core, s, m):
        here, _, dev = messages(core, s)[m]
        remote(here, here, g_send.at[s, m], g_recv.at[s, m], dev).wait_recv()

    def sent(core, s, m):
        _, src, dev = messages(core, s)[m]
        remote(src, src, g_send.at[s, m], g_recv.at[s, m], dev).wait_send()

    def ring_stage(core, s, k):
        if k > 0:
            got(core, s, 2 * k - 2)
            got(core, s, 2 * k - 1)
        if k < 6:
            send(core, s, 2 * k)
            send(core, s, 2 * k + 1)
        else:
            half = wb.at[core, s]
            remote(half, half, sib_send.at[s], sib_recv.at[s], sib).start()

    def has(core, s):
        return (s != 1) if core == 0 else True

    def expander(g, rows, kind):
        i = lax.broadcasted_iota(jnp.int32, (rows, 256), 0)
        j = lax.broadcasted_iota(jnp.int32, (rows, 256), 1)
        head = 2 * g + 20 * (j >> 7) + ((j >> 6) & 1)
        return jnp.where((i & 127) == head, 1.0, 0.0).astype(kind)

    def project(w):
        mixed = dot(tokv[...], w)
        v = valid[...]
        for half in range(2):
            part = mixed[:, half * 128 : half * 128 + 128] * v
            conv[half] = part.astype(BF16).astype(F32)

    def convolve(half, j, tile):
        lanes = pl.ds(pl.multiple_of(tile * 128, 128), 128)
        acc = jnp.broadcast_to(vec_ref[pl.ds(tile, 1), :], (CH, 128))
        for k in range(4):
            acc = acc + cw_ref[k : k + 1, lanes] * conv[half, pl.ds(13 + k + CH * j, CH), :]
        acc = 0.5 * acc
        return (acc + acc * jnp.tanh(acc)).astype(BF16)

    def halves(v):
        top = v.astype(BF16)
        low = (v - top.astype(F32)).astype(BF16)
        return top, low

    ri = lax.broadcasted_iota(jnp.int32, (CH, CH), 0)
    ci = lax.broadcasted_iota(jnp.int32, (CH, CH), 1)

    def prepare():
        tok_copy.wait()
        halo.wait_send()
        halo.wait_recv()
        raw = dot(tokv[pl.ds(HALO, SPAN), :], wb[0, 0].reshape(D, 128))
        project(jnp.concatenate([wb[1, 0].reshape(D, 128), wb[1, 1].reshape(D, 128)], axis=1))
        tri = jnp.where(ri >= ci, 1.0, 0.0)
        before = jnp.zeros((1, 128), F32)
        for j in range(NCH):
            rows = slice(j * CH, (j + 1) * CH)
            b = convolve(0, j, 20)
            cj = convolve(1, j, 21)
            cc[j] = jnp.concatenate([cj, cj], axis=1)
            bt[j] = b.astype(F32).T.astype(BF16)
            score = lax.dot_general(cj, b, (((1,), (1,)), ((), ())), preferred_element_type=F32)
            sc[j] = jnp.where(ri >= ci, score, 0.0)
            v = raw[rows] + vec_ref[42:43, :]
            step = jnp.maximum(v, 0.0) + jnp.log1p(jnp.exp(-jnp.abs(v)))
            step = step * valid[pl.ds(HALO + j * CH, CH), :]
            total = dot(tri, -step * vec_ref[43:44, :], precision=HIGH)
            cum[pl.ds(j * CH, CH), :] = total * LOG2E
            cum_t[j] = ((total - jnp.log(step)) * LOG2E).T
            end = total[CH - 1 : CH, :]
            top, low = halves(jnp.exp(end - total) * step)
            wk[pl.ds(j * CH, CH), :] = jnp.concatenate([top, low], axis=1)
            top, low = halves(jnp.exp(total))
            ec[pl.ds(j * CH, CH), :] = jnp.concatenate([top, low], axis=1)
            dcw[j : j + 1, :] = jnp.exp(end)
            dcw[4 + j : 5 + j, :] = jnp.exp(before)
            before = before + end
        dcw[8:9, :] = vec_ref[44:45, :]
        ta[q] = jnp.broadcast_to(before, (8, 128))
        for d in range(1, 8):
            remote(ta.at[q], ta.at[q], t_send.at[d - 1], t_recv.at[d - 1], qn[d]).start()

    def link_decays():
        for d in range(1, 8):
            src = (q - d) % 8
            remote(ta.at[src], ta.at[src], t_send.at[d - 1], t_recv.at[d - 1], qn[d]).wait_recv()
        tot = [ta[d][0:1, :] for d in range(8)]
        dcw[16:24, :] = jnp.zeros((8, 128), F32)
        def between(lower, upper):
            acc = jnp.zeros((1, 128), F32)
            for d in range(8):
                acc = acc + tot[d] * jnp.where((d >= lower) & (d < upper), 1.0, 0.0)
            return jnp.exp(acc)

        for m in range(1, 4):
            xs = (x - m) % 4
            dcw[15 + m : 16 + m, :] = between(2 * xs + 2, 2 * x) * jnp.where(xs < x, 1.0, 0.0)
            dcw[20 + m : 21 + m, :] = between(2 * xs + 2, 8)
        dcw[9:10, :] = between(2 * x + 2, 8)
        dcw[19:20, :] = jnp.exp(ta[2 * x][0:1, :])
        dcw[20:21, :] = jnp.exp(ta[2 * x + 1][0:1, :])

    lane = lax.broadcasted_iota(jnp.int32, (CH, 128), 1)

    def group(g):
        s = g + 2
        project(jnp.concatenate([wb[0, s].reshape(D, 128), wb[1, s].reshape(D, 128)], axis=1))
        spread = expander(g, 256, BF16)
        decays = dot(dcw[...], expander(g, 128, F32), precision=HIGH)
        dx[g] = decays
        cums = cum[...]
        for j in range(NCH):
            xj = [convolve(half, j, g + 10 * half) for half in range(2)]
            weight = dot(wk[pl.ds(j * CH, CH), :], spread)
            xf = jnp.concatenate(xj, axis=1).astype(F32)
            local = dot(bt[j], (weight * xf).astype(BF16))
            if j > 0:
                local = local + decays[j : j + 1, :] * lb[g, j - 1]
            if j < NCH - 1:
                lb[g, j] = local
            else:
                dst[g] = local
            for half in range(2):
                mix = []
                for e in range(2):
                    h = 20 * half + e
                    cq = jnp.broadcast_to(cums[j * CH : (j + 1) * CH, h : h + 1], (CH, CH))
                    ck = cum_t[j, pl.ds(2 * g + h, 1), :]
                    mix.append((jnp.exp2(jnp.minimum(cq - ck, 100.0)) * sc[j]).astype(BF16))
                zero = jnp.zeros_like(xj[half])
                pair = jnp.concatenate(
                    [jnp.where(lane < 64, xj[half], zero), jnp.where(lane < 64, zero, xj[half])],
                    axis=0,
                )
                inner = dot(jnp.concatenate(mix, axis=1), pair)
                lanes = slice(half * 128, half * 128 + 128)
                skip = decays[8:9, lanes]
                out[g, pl.ds(j * CH, CH), lanes] = inner + skip * xj[half].astype(F32)
        cum[...] = pltpu.roll(cums, 126, 1)

        @pl.when(c == 0)
        def _():
            remote(dst.at[g], d0.at[g], d_send.at[g], d_recv.at[g], sib).start()

    def total_copy(g, m):
        return remote(
            tb.at[g], tr.at[m - 1, g], x_send.at[m - 1, g], x_recv.at[m - 1, g], qn[2 * m]
        )

    def chip_total(g):
        @pl.when(c == 1)
        def _():
            remote(dst.at[g], d0.at[g], d_send.at[g], d_recv.at[g], sib).wait_recv()
            tb[g] = (dx[g, 20:21, :] * d0[g] + dst[g]).astype(BF16)
            for m in range(1, 4):
                total_copy(g, m).start()

    def own_state():
        return remote(fd.at[0], zg.at[z], f_send, f_recv, sib)

    def chip_entry(g):
        @pl.when(c == 1)
        def _():
            for m in range(1, 4):
                total_copy(g, m).wait_recv()
            parts = [tr[m, g].astype(F32) for m in range(3)]
            entry = dx[g, 16:17, :] * parts[0] + dx[g, 17:18, :] * parts[1]
            ib[g] = entry + dx[g, 18:19, :] * parts[2]
            remote(ib.at[g], ib.at[g], i_send.at[g], i_recv.at[g], sib).start()
            for half in range(2):
                head = 20 * half + 2 * g
                lanes = slice(half * 128, half * 128 + 128)
                chips = [(head + e) // 10 for e in range(2)]

                @pl.when((chips[0] == x) | (chips[1] == x))
                def _():
                    leaving = dx[g, 9:10, lanes] * tb[g, :, lanes].astype(F32)
                    for m in range(3):
                        leaving += dx[g, 21 + m : 22 + m, lanes] * tr[m, g, :, lanes].astype(F32)
                    turned = leaving.T.reshape(2, 64, 128).astype(BF16)
                    for e in range(2):
                        @pl.when(chips[e] == x)
                        def _():
                            fd[((head + e) // 5) % 2, (head + e) % 5] = turned[e]

            @pl.when(g == 2 + 5 * (x % 2))
            def _():
                own_state().start()

            @pl.when(g == 4 + 5 * (x % 2))
            def _():
                zg[z] = fd[1]

    def late(g):
        spread = expander(g, 256, BF16)

        @pl.when(c == 0)
        def _():
            remote(ib.at[g], ib.at[g], i_send.at[g], i_recv.at[g], sib).wait_recv()
            d0[g] = ib[g]

        @pl.when(c == 1)
        def _():
            d0[g] = d0[g] + dx[g, 19:20, :] * ib[g]

        incoming = d0[g]
        for j in range(NCH):
            entry = dx[g, 4 + j : 5 + j, :] * incoming
            if j > 0:
                entry = entry + lb[g, j - 1]
            carried = dot(cc[j], jnp.concatenate(halves(entry), axis=0))
            carried = carried * dot(ec[pl.ds(j * CH, CH), :], spread)
            full = out[g, pl.ds(j * CH, CH), :] + carried
            out[g, pl.ds(j * CH, CH), :] = full
            square = full * full
            ssq[pl.ds(j * CH, CH), :] += square[:, :128] + square[:, 128:]

    def zroute(m, here):
        heads = [pl.ds(0, 5)] * 6 + [pl.ds(0, 3), pl.ds(3, 2)]
        dz = ([7, 1, 6, 2, 5, 3, 4, 4] if here else [0, 0, 7, 1, 6, 2, 5, 3])[m]
        ref = zg.at[zi[dz], heads[m]]
        return remote(ref, ref, z_send.at[m], z_recv.at[m], zp if m % 2 == 0 else zm)

    def y_copy(dy):
        return remote(ys.at[dy - 1], yr.at[dy], y_send.at[dy - 1], y_recv.at[dy - 1], yn[dy])

    def route(k):
        if k == 0:
            @pl.when(c == 0)
            def _():
                own_state().wait_recv()
        elif k < 5:
            zroute(2 * k - 2, True).wait_recv()
            zroute(2 * k - 1, True).wait_recv()
        if k < 4:
            zroute(2 * k, False).start()
            zroute(2 * k + 1, False).start()
        elif k == 4:
            for dy in range(1, 4):
                ys[dy - 1] = zg[hold[dy] // 4]
                y_copy(dy).start()
            yr[0] = zg[hold[0] // 4]
        else:
            for dy in range(1, 4):
                y_copy(dy).wait_recv()
            fin_ref[...] = yr[(y + 4 - hold[0] % 4) % 4].astype(F32)

    def normed(j):
        rows = pl.ds(j * CH, CH)
        mean = jnp.sum(ssq[rows, :], axis=1, keepdims=True) * (1.0 / D)
        factor = lax.rsqrt(mean + EPS) * valid[pl.ds(HALO + j * CH, CH), :][:, 0:1]
        for g in range(GROUPS):
            for half in range(2):
                tile = g + 10 * half
                gain = vec_ref[22 + tile : 23 + tile, :]
                part = out[g, rows, 128 * half : 128 * half + 128] * factor * gain
                resv[rows, 128 * tile : 128 * tile + 128] = part.astype(BF16)
        out_copy(j).start()

    def out_copy(j):
        rows = pl.ds(j * CH, CH)
        return pltpu.make_async_copy(resv.at[rows], res_hbm.at[rows], o_sem.at[j])

    def body(t, carry):
        for k in range(7):
            s = t - GAP * k
            @pl.when((s >= (0 if k else 2)) & (s < SLOTS))
            def _():
                @pl.when((c == 0) & has(0, s))
                def _():
                    ring_stage(0, s, k)

                @pl.when(c == 1)
                def _():
                    ring_stage(1, s, k)
        s = t - LAG
        @pl.when((s >= 0) & (s < SLOTS))
        def _():
            @pl.when(c == 0)
            def _():
                half = wb.at[1, s]
                remote(half, half, sib_send.at[s], sib_recv.at[s], sib).wait_recv()

            @pl.when((c == 1) & has(0, s))
            def _():
                half = wb.at[0, s]
                remote(half, half, sib_send.at[s], sib_recv.at[s], sib).wait_recv()

        g = s - 2

        @pl.when(g == -1)
        def _():
            prepare()

        @pl.when(g == 0)
        def _():
            link_decays()

        @pl.when((g >= 0) & (g < GROUPS))
        def _():
            group(g)

        @pl.when((g >= TO_TOTAL) & (g < GROUPS + TO_TOTAL))
        def _():
            chip_total(g - TO_TOTAL)

        @pl.when((g >= TO_ENTRY) & (g < GROUPS + TO_ENTRY))
        def _():
            chip_entry(g - TO_ENTRY)

        for k in range(6):
            @pl.when(g == TO_ENTRY + 3 + 2 * c + 5 * (x % 2) + k)
            def _():
                route(k)

        @pl.when((g >= TO_LATE) & (g < GROUPS + TO_LATE))
        def _():
            late(g - TO_LATE)

        for j in range(NCH):
            @pl.when(g == GROUPS + TO_LATE + j)
            def _():
                normed(j)

        return carry

    assemble(0, range(2))
    for s in range(2):
        for core in range(2):
            if core == 1 or s != 1:
                @pl.when(c == core)
                def _():
                    ring_stage(core, s, 0)
    assemble(1, range(2, SLOTS))
    lax.fori_loop(0, LAG + 2 + GROUPS + TO_LATE + 4, body, 0)

    for copies in w_copies:
        for copy in copies[1:]:
            copy.wait_send()
    for dy in range(1, 4):
        y_copy(dy).wait_send()
    for m in range(8):
        zroute(m, False).wait_send()
    for j in range(NCH):
        out_copy(j).wait()
    for d in range(1, 8):
        remote(ta.at[q], ta.at[q], t_send.at[d - 1], t_recv.at[d - 1], qn[d]).wait_send()

    def drain_slot(s, carry):
        for core in range(2):
            @pl.when((c == core) & has(core, s))
            def _():
                for m in range(12):
                    sent(core, s, m)
                half = wb.at[core, s]
                remote(half, half, sib_send.at[s], sib_recv.at[s], sib).wait_send()
        return carry

    lax.fori_loop(0, SLOTS, drain_slot, 0)

    def drain_group(g, carry):
        @pl.when(c == 0)
        def _():
            remote(dst.at[g], d0.at[g], d_send.at[g], d_recv.at[g], sib).wait_send()

        @pl.when(c == 1)
        def _():
            remote(ib.at[g], ib.at[g], i_send.at[g], i_recv.at[g], sib).wait_send()
            for m in range(1, 4):
                total_copy(g, m).wait_send()
        return carry

    lax.fori_loop(0, GROUPS, drain_group, 0)

    @pl.when(c == 1)
    def _():
        own_state().wait_send()


def on_device(
    tokens, mix_weight, step_weight, conv_weight, conv_bias, step_bias, decay_rate,
    skip_gain, norm_gain, prompt_len, prompt_start, deal,
):
    heads = decay_rate.shape[0]
    gap = jnp.zeros((128 - heads,), F32)
    vec = jnp.concatenate(
        [conv_bias, norm_gain, step_bias, gap, decay_rate, gap, skip_gain, gap, jnp.zeros((384,), F32)]
    ).reshape(48, 128)

    vm, dma = pltpu.VMEM, pltpu.SemaphoreType.DMA
    vspec = pl.BlockSpec(memory_space=pltpu.VMEM)
    sspec = pl.BlockSpec(memory_space=pltpu.SMEM)
    aspec = pl.BlockSpec(memory_space=pl.ANY)
    result, final = pl.pallas_call(
        kernel,
        out_shape=(
            jax.ShapeDtypeStruct((SPAN, D), BF16),
            jax.ShapeDtypeStruct((5, 64, 128), F32),
        ),
        in_specs=[aspec, vspec, vspec, vspec, vspec, sspec, sspec, sspec],
        out_specs=(aspec, vspec),
        scratch_shapes=[
            vm((2, SLOTS, 8, 4, 80, 128), BF16),
            vm((2, 16, 1536), BF16),
            vm((8, 16, 1536), BF16),
            vm((SPAN + HALO, D), BF16),
            vm((SPAN + HALO, 128), F32),
            vm((2, SPAN + HALO, 128), F32),
            pltpu.SMEM((4,), jnp.int32),
            vm((GROUPS, SPAN, 256), F32),
            vm((SPAN, D), BF16),
            vm((SPAN, 128), F32),
            vm((NCH, 128, CH), F32),
            vm((SPAN, 256), BF16),
            vm((SPAN, 256), BF16),
            vm((NCH, CH, CH), F32),
            vm((NCH, 128, CH), BF16),
            vm((NCH, CH, 256), BF16),
            vm((24, 128), F32),
            vm((GROUPS, 24, 256), F32),
            vm((8, 8, 128), F32),
            vm((GROUPS, 3, 128, 256), F32),
            vm((GROUPS, 128, 256), F32),
            vm((GROUPS, 128, 256), F32),
            vm((GROUPS, 128, 256), BF16),
            vm((3, GROUPS, 128, 256), BF16),
            vm((GROUPS, 128, 256), F32),
            vm((2, 5, 64, 128), BF16),
            vm((8, 5, 64, 128), BF16),
            vm((3, 5, 64, 128), BF16),
            vm((4, 5, 64, 128), BF16),
            vm((SPAN, 128), F32),
            dma((2, 7)), dma((2, 8)), dma((2,)), dma,
            dma((SLOTS, 12)), dma((SLOTS, 12)), dma((SLOTS,)), dma((SLOTS,)),
            dma((7,)), dma((7,)), dma((GROUPS,)), dma((GROUPS,)),
            dma((3, GROUPS)), dma((3, GROUPS)), dma((GROUPS,)), dma((GROUPS,)),
            dma, dma, dma((8,)), dma((8,)), dma((3,)), dma((3,)), dma((NCH,)),
        ],
        compiler_params=pltpu.CompilerParams(
            collective_id=0, has_side_effects=True, vmem_limit_bytes=62 * 1024 * 1024
        ),
    )(tokens[0], mix_weight, step_weight, conv_weight, vec, prompt_len, prompt_start, deal)
    return (result[None], final[None])


def solution(mesh):
    return jax.shard_map(
        on_device,
        mesh=mesh,
        in_specs=(P("req", "seq", None), P(("req", "seq"), None), P(("req", "seq"), None))
        + (P(),) * 9,
        out_specs=(P("req", "seq", None), P("req", "seq", None, None)),
        check_vma=False,
    )
```

time: 135 us -> 118 us (0.87)
  Pallas kernels: 120 us -> 112 us
  local copies, waits for them, and re-layouts: 10.6 us -> 5.52 us
  other arithmetic: 2.67 us -> 0 us
    pallas_call x1, Pallas kernels: 120 us -> 112 us  [on_device(): pl.pallas_call(kernel, out_shape=(jax.ShapeDtypeStruct((SPAN, D), BF16),...]
    slice x6 -> x0, local copies, waits for them, and re-layouts: 2.25 us -> none  [the longest x1 0.78 us: on_device(): conv_weight[:, :2560]]
    another operation x2 -> x0, other arithmetic: 1.93 us -> none  [the longest x1 1.27 us: on_device(): hv = jnp.pad(jnp.stack([step_bias, decay_rate]), ((0, 6), (0, 128 - heads)))]
    broadcast_in_dim x5 -> x2, local copies, waits for them, and re-layouts: 1.59 us -> 0.01 us  [the longest x1 0.01 us: on_device(): jnp.zeros((384,), F32)]
where the time goes in v2:
time: 118 us
  Pallas kernels  112 us (95%)
  local copies, waits for them, and re-layouts  5.52 us (5%)
    pallas_call x1, Pallas kernels, on_device(): pl.pallas_call(kernel, out_shape=(jax.ShapeDtypeStruct((SPAN, D), BF16),...  112 us
    unnamed x4, local copies, waits for them, and re-layouts  4.11 us

profile of v2, /device:TPU:2, one launch (start us, length us, event | category | flops | bytes accessed | tf_op | source)
XLA Modules:
  0.0 117.8 jit_solution(17073852095889549372)
XLA Ops:
  0.6 1.4 %concatenate.3 = f32[6144]{0:T(1024)} concatenate(f32[2816]{0:T(1024)} %param.16, f32[2560]{0:T(1024)} %param.20, f32[40]{0:T(128)} %param.17, f32[88]{0:T(128)S(1)} %broadcast_in_dim.12, f32[40]{0:T(128)} %param.18, f32[88]{0:T(128)S(1)} %broadcast_in_dim.12, f32[40]{0:T(128)} %param.19, f32[88]{0:T(128)S(1)} %broadcast_in_dim.12, f32[384]{0:T(512)S(1)} %broadcast_in_dim.13), dimensions={0} | concatenate | bytes 49152 | tf_op jit(solution)/shard_map/concatenate | solution.py:559
  2.1 111.7 %shard_map.131 = (bf16[512,2560]{1,0:T(8,128)(2,1)}, f32[5,64,128]{2,1,0:T(8,128)}) custom-call(bf16[512,2560]{1,0:T(8,128)(2,1)} %bitcast.4, bf16[10,2816]{1,0:T(8,128)(2,1)} %mix_ref.1, bf16[10,40]{1,0:T(8,128)(2,1)} %sw_ref.1, f32[4,2816]{1,0:T(4,128)} %cw_ref.1, f32[48,128]{1,0:T(8,128)} %bitcast.7, s32[32]{0:T(128)} %len_s.1, s32[32]{0:T(128)} %start_s.1, ...), custom_call_target="tpu_custom_call" | custom-call | tf_op jit(solution)/shard_map/pallas_call | solution.py:567
  113.7 0.0 copy-start
  113.7 3.4 %copy.16 = bf16[1,512,2560]{2,1,0:T(8,128)(2,1)} copy(bf16[1,512,2560]{2,1,0:T(8,128)(2,1)} %bitcast.5) | data formatting | bytes 5242880
  117.2 0.0 copy-done
  117.2 0.7 copy.17
  (2 shorter events, 0.0 us)
Async XLA Ops:
  113.7 3.5 %copy-start = (f32[5,64,128]{2,1,0:T(8,128)S(1)}, f32[5,64,128]{2,1,0:T(8,128)}, u32[]{:S(2)}) copy-start(f32[5,64,128]{2,1,0:T(8,128)} %get-tuple-element.5) | copy-start | bytes 491524

commit v3 on v2

--- a/solution.py
+++ b/solution.py
@@ -31,12 +31,12 @@
 
 def kernel(
     tok_hbm, mix_ref, sw_ref, cw_ref, vec_ref, len_s, start_s, deal_s,
-    res_hbm, fin_ref,
-    wb, wl_ref, stage, tokv, valid, conv, hold, out, resv, cum, cum_t, wk, ec, sc, bt, cc,
+    res_ref, fin_ref,
+    wb, wl_ref, stage, tokv, valid, conv, hold, out, cum, cum_t, wk, ec, sc, bt, cc,
     dcw, dx, ta, lb, dst, d0, tb, tr, ib, fd, zg, ys, yr, ssq,
     w_send, w_recv, h_sem, tok_sem, g_send, g_recv, sib_send, sib_recv,
     t_send, t_recv, d_send, d_recv, x_send, x_recv, i_send, i_recv,
-    f_send, f_recv, z_send, z_recv, y_send, y_recv, o_sem,
+    f_send, f_recv, z_send, z_recv, y_send, y_recv,
 ):
     r, q = lax.axis_index("req"), lax.axis_index("seq")
     z, y, x, c = r // 4, r % 4, q // 2, q % 2
@@ -427,12 +427,8 @@
                 tile = g + 10 * half
                 gain = vec_ref[22 + tile : 23 + tile, :]
                 part = out[g, rows, 128 * half : 128 * half + 128] * factor * gain
-                resv[rows, 128 * tile : 128 * tile + 128] = part.astype(BF16)
-        out_copy(j).start()
-
-    def out_copy(j):
-        rows = pl.ds(j * CH, CH)
-        return pltpu.make_async_copy(resv.at[rows], res_hbm.at[rows], o_sem.at[j])
+                res_ref[rows, 128 * tile : 128 * tile + 128] = part.astype(BF16)
+
 
     def body(t, carry):
         for k in range(7):
@@ -514,8 +510,6 @@
         y_copy(dy).wait_send()
     for m in range(8):
         zroute(m, False).wait_send()
-    for j in range(NCH):
-        out_copy(j).wait()
     for d in range(1, 8):
         remote(ta.at[q], ta.at[q], t_send.at[d - 1], t_recv.at[d - 1], qn[d]).wait_send()
 
@@ -567,11 +561,11 @@
     result, final = pl.pallas_call(
         kernel,
         out_shape=(
-            jax.ShapeDtypeStruct((SPAN, D), BF16),
-            jax.ShapeDtypeStruct((5, 64, 128), F32),
+            pltpu.VMEM((SPAN, D), BF16),
+            pltpu.VMEM((5, 64, 128), F32),
         ),
         in_specs=[aspec, vspec, vspec, vspec, vspec, sspec, sspec, sspec],
-        out_specs=(aspec, vspec),
+        out_specs=(vspec, vspec),
         scratch_shapes=[
             vm((2, SLOTS, 8, 4, 80, 128), BF16),
             vm((2, 16, 1536), BF16),
@@ -581,7 +575,6 @@
             vm((2, SPAN + HALO, 128), F32),
             pltpu.SMEM((4,), jnp.int32),
             vm((GROUPS, SPAN, 256), F32),
-            vm((SPAN, D), BF16),
             vm((SPAN, 128), F32),
             vm((NCH, 128, CH), F32),
             vm((SPAN, 256), BF16),
@@ -607,10 +600,10 @@
             dma((SLOTS, 12)), dma((SLOTS, 12)), dma((SLOTS,)), dma((SLOTS,)),
             dma((7,)), dma((7,)), dma((GROUPS,)), dma((GROUPS,)),
             dma((3, GROUPS)), dma((3, GROUPS)), dma((GROUPS,)), dma((GROUPS,)),
-            dma, dma, dma((8,)), dma((8,)), dma((3,)), dma((3,)), dma((NCH,)),
+            dma, dma, dma((8,)), dma((8,)), dma((3,)), dma((3,)),
         ],
         compiler_params=pltpu.CompilerParams(
-            collective_id=0, has_side_effects=True, vmem_limit_bytes=62 * 1024 * 1024
+            collective_id=0, has_side_effects=True, vmem_limit_bytes=52 * 1024 * 1024
         ),
     )(tokens[0], mix_weight, step_weight, conv_weight, vec, prompt_len, prompt_start, deal)
     return (result[None], final[None])

time: 118 us -> 115 us (0.975)
  Pallas kernels: 112 us -> 110 us
  local copies, waits for them, and re-layouts: 5.52 us -> 3.57 us
    unnamed x4 -> x2, local copies, waits for them, and re-layouts: 4.11 us -> 2.16 us
    pallas_call x1, Pallas kernels: 112 us -> 110 us  [on_device(): pl.pallas_call(kernel, out_shape=(pltpu.VMEM((SPAN, D), BF16), pltpu.VMEM...]
where the time goes in v3:
time: 115 us; the launch traced here: 114 us
  Pallas kernels  110 us (96%)
  local copies, waits for them, and re-layouts  3.57 us (3%)
    pallas_call x1, Pallas kernels, on_device(): pl.pallas_call(kernel, out_shape=(pltpu.VMEM((SPAN, D), BF16), pltpu.VMEM...  110 us

profile of v3, /device:TPU:2, one launch (start us, length us, event | category | flops | bytes accessed | tf_op | source)
XLA Modules:
  0.0 114.4 jit_solution(9232805759901685788)
XLA Ops:
  0.6 1.4 %concatenate.3 = f32[6144]{0:T(1024)} concatenate(f32[2816]{0:T(1024)} %param.16, f32[2560]{0:T(1024)} %param.20, f32[40]{0:T(128)} %param.17, f32[88]{0:T(128)S(1)} %broadcast_in_dim.12, f32[40]{0:T(128)} %param.18, f32[88]{0:T(128)S(1)} %broadcast_in_dim.12, f32[40]{0:T(128)} %param.19, f32[88]{0:T(128)S(1)} %broadcast_in_dim.12, f32[384]{0:T(512)S(1)} %broadcast_in_dim.13), dimensions={0} | concatenate | bytes 49152 | tf_op jit(solution)/shard_map/concatenate | solution.py:553
  2.1 110.2 %shard_map.131 = (bf16[512,2560]{1,0:T(8,128)(2,1)S(1)}, f32[5,64,128]{2,1,0:T(8,128)S(1)}) custom-call(bf16[512,2560]{1,0:T(8,128)(2,1)} %bitcast.6, bf16[10,2816]{1,0:T(8,128)(2,1)} %mix_ref.1, bf16[10,40]{1,0:T(8,128)(2,1)} %sw_ref.1, f32[4,2816]{1,0:T(4,128)} %cw_ref.1, f32[48,128]{1,0:T(8,128)} %bitcast.7, s32[32]{0:T(128)} %len_s.1, s32[32]{0:T(128)} %start_s.1, ...), custom_call_target="tpu_custom_call" | custom-call | tf_op jit(solution)/shard_map/pallas_call | solution.py:561
  112.3 1.5 %copy.16 = bf16[1,512,2560]{2,1,0:T(8,128)(2,1)} copy(bf16[1,512,2560]{2,1,0:T(8,128)(2,1)S(1)} %bitcast.4) | data formatting | bytes 5242880
  113.8 0.7 copy.17
  (2 shorter events, 0.0 us)

commit v4 on v3

--- a/solution.py
+++ b/solution.py
@@ -30,9 +30,9 @@
 
 
 def kernel(
-    tok_hbm, mix_ref, sw_ref, cw_ref, vec_ref, len_s, start_s, deal_s,
+    tok_hbm, mix_ref, sw_ref, cw_ref, cb_ref, ng_ref, sb_ref, dr_ref, sg_ref, len_s, start_s, deal_s,
     res_ref, fin_ref,
-    wb, wl_ref, stage, tokv, valid, conv, hold, out, cum, cum_t, wk, ec, sc, bt, cc,
+    wb, wl_ref, stage, tokv, valid, conv, hold, hv, out, cum, cum_t, wk, ec, sc, bt, cc,
     dcw, dx, ta, lb, dst, d0, tb, tr, ib, fd, zg, ys, yr, ssq,
     w_send, w_recv, h_sem, tok_sem, g_send, g_recv, sib_send, sib_recv,
     t_send, t_recv, d_send, d_recv, x_send, x_recv, i_send, i_recv,
@@ -60,6 +60,9 @@
         pl.semaphore_signal(barrier, inc=1, device_id=dev, device_id_type=MESH)
     tok_copy = pltpu.make_async_copy(tok_hbm, tokv.at[pl.ds(HALO, SPAN)], tok_sem)
     tok_copy.start()
+    hv[...] = jnp.zeros_like(hv)
+    for n, ref in enumerate((sb_ref, dr_ref, sg_ref)):
+        hv[n : n + 1, 0:40] = ref[...]
     wl_ref[...] = jnp.zeros_like(wl_ref)
     wl_ref[0, 0:10, 0:40] = sw_ref[...]
     wl_ref[0, 0:10, 256:1536] = mix_ref[:, 0:1280]
@@ -204,7 +207,7 @@
 
     def convolve(half, j, tile):
         lanes = pl.ds(pl.multiple_of(tile * 128, 128), 128)
-        acc = jnp.broadcast_to(vec_ref[pl.ds(tile, 1), :], (CH, 128))
+        acc = jnp.broadcast_to(cb_ref[pl.ds(tile, 1), :], (CH, 128))
         for k in range(4):
             acc = acc + cw_ref[k : k + 1, lanes] * conv[half, pl.ds(13 + k + CH * j, CH), :]
         acc = 0.5 * acc
@@ -234,10 +237,10 @@
             bt[j] = b.astype(F32).T.astype(BF16)
             score = lax.dot_general(cj, b, (((1,), (1,)), ((), ())), preferred_element_type=F32)
             sc[j] = jnp.where(ri >= ci, score, 0.0)
-            v = raw[rows] + vec_ref[42:43, :]
+            v = raw[rows] + hv[0:1, :]
             step = jnp.maximum(v, 0.0) + jnp.log1p(jnp.exp(-jnp.abs(v)))
             step = step * valid[pl.ds(HALO + j * CH, CH), :]
-            total = dot(tri, -step * vec_ref[43:44, :], precision=HIGH)
+            total = dot(tri, -step * hv[1:2, :], precision=HIGH)
             cum[pl.ds(j * CH, CH), :] = total * LOG2E
             cum_t[j] = ((total - jnp.log(step)) * LOG2E).T
             end = total[CH - 1 : CH, :]
@@ -248,7 +251,7 @@
             dcw[j : j + 1, :] = jnp.exp(end)
             dcw[4 + j : 5 + j, :] = jnp.exp(before)
             before = before + end
-        dcw[8:9, :] = vec_ref[44:45, :]
+        dcw[8:9, :] = hv[2:3, :]
         ta[q] = jnp.broadcast_to(before, (8, 128))
         for d in range(1, 8):
             remote(ta.at[q], ta.at[q], t_send.at[d - 1], t_recv.at[d - 1], qn[d]).start()
@@ -425,7 +428,7 @@
         for g in range(GROUPS):
             for half in range(2):
                 tile = g + 10 * half
-                gain = vec_ref[22 + tile : 23 + tile, :]
+                gain = ng_ref[tile : tile + 1, :]
                 part = out[g, rows, 128 * half : 128 * half + 128] * factor * gain
                 res_ref[rows, 128 * tile : 128 * tile + 128] = part.astype(BF16)
 
@@ -548,11 +551,8 @@
     tokens, mix_weight, step_weight, conv_weight, conv_bias, step_bias, decay_rate,
     skip_gain, norm_gain, prompt_len, prompt_start, deal,
 ):
-    heads = decay_rate.shape[0]
-    gap = jnp.zeros((128 - heads,), F32)
-    vec = jnp.concatenate(
-        [conv_bias, norm_gain, step_bias, gap, decay_rate, gap, skip_gain, gap, jnp.zeros((384,), F32)]
-    ).reshape(48, 128)
+    rows = [conv_bias.reshape(22, 128), norm_gain.reshape(20, 128)]
+    rows += [v.reshape(1, 40) for v in (step_bias, decay_rate, skip_gain)]
 
     vm, dma = pltpu.VMEM, pltpu.SemaphoreType.DMA
     vspec = pl.BlockSpec(memory_space=pltpu.VMEM)
@@ -564,7 +564,7 @@
             pltpu.VMEM((SPAN, D), BF16),
             pltpu.VMEM((5, 64, 128), F32),
         ),
-        in_specs=[aspec, vspec, vspec, vspec, vspec, sspec, sspec, sspec],
+        in_specs=[aspec] + [vspec] * 8 + [sspec, sspec, sspec],
         out_specs=(vspec, vspec),
         scratch_shapes=[
             vm((2, SLOTS, 8, 4, 80, 128), BF16),
@@ -574,6 +574,7 @@
             vm((SPAN + HALO, 128), F32),
             vm((2, SPAN + HALO, 128), F32),
             pltpu.SMEM((4,), jnp.int32),
+            vm((8, 128), F32),
             vm((GROUPS, SPAN, 256), F32),
             vm((SPAN, 128), F32),
             vm((NCH, 128, CH), F32),
@@ -605,7 +606,7 @@
         compiler_params=pltpu.CompilerParams(
             collective_id=0, has_side_effects=True, vmem_limit_bytes=52 * 1024 * 1024
         ),
-    )(tokens[0], mix_weight, step_weight, conv_weight, vec, prompt_len, prompt_start, deal)
+    )(tokens[0], mix_weight, step_weight, conv_weight, *rows, prompt_len, prompt_start, deal)
     return (result[None], final[None])
 
 

time: 115 us -> 113 us (0.983)
  local copies, waits for them, and re-layouts: 3.57 us -> 2.16 us
    concatenate x1 -> x0, local copies, waits for them, and re-layouts: 1.41 us -> none  [on_device(): jnp.concatenate([conv_bias, norm_gain, step_bias, gap, decay_rate, gap, s...]
where the time goes in v4:
time: 113 us
  Pallas kernels  110 us (97%)
  local copies, waits for them, and re-layouts  2.16 us (2%)
    pallas_call x1, Pallas kernels, on_device(): pl.pallas_call(kernel, out_shape=(pltpu.VMEM((SPAN, D), BF16), pltpu.VMEM...  110 us

profile of v4, /device:TPU:2, one launch (start us, length us, event | category | flops | bytes accessed | tf_op | source)
XLA Modules:
  0.0 113.1 jit_solution(7879332950005160872)
XLA Ops:
  0.6 110.3 %shard_map.131 = (bf16[512,2560]{1,0:T(8,128)(2,1)S(1)}, f32[5,64,128]{2,1,0:T(8,128)S(1)}) custom-call(bf16[512,2560]{1,0:T(8,128)(2,1)} %bitcast.10, bf16[10,2816]{1,0:T(8,128)(2,1)} %mix_ref.1, bf16[10,40]{1,0:T(8,128)(2,1)} %sw_ref.1, f32[4,2816]{1,0:T(4,128)} %cw_ref.1, f32[22,128]{1,0:T(8,128)} %bitcast.11, f32[20,128]{1,0:T(8,128)} %bitcast.12, ...), custom_call_target="tpu_custom_call" | custom-call | tf_op jit(solution)/shard_map/pallas_call | solution.py:561
  111.0 1.5 %copy.16 = bf16[1,512,2560]{2,1,0:T(8,128)(2,1)} copy(bf16[1,512,2560]{2,1,0:T(8,128)(2,1)S(1)} %bitcast.8) | data formatting | bytes 5242880
  112.4 0.7 copy.17
